TPU v7x, 32 devices: a whole 2x2x4 slice. The times are simulated.
32 devices in a mesh: gx: 4 (over z), gy: 4 (over y, x), gz: 2 (over core).
Axes of the slice: x: 2, y: 2, z: 4, core: 2. Of those that a mesh axis runs over, the one named last changes fastest.
Arguments:
- source_points: float32 [3, 13, 4, 16, 4, 512], P(None, None, 'gx', 'gy', 'gz'), may hold values from -3 to 3
- target_points: float32 [3, 13, 4, 16, 4, 512], P(None, None, 'gx', 'gy', 'gz'), may hold values from -3 to 3
- normals: float32 [3, 13, 4, 16, 4, 512], P(None, None, 'gx', 'gy', 'gz'), may hold values from -4 to 4
- weights: float32 [13, 4, 16, 4, 512], P(None, 'gx', 'gy', 'gz'), may hold values from 0.1 to 1
- blocks: int32 [13, 4, 16, 4], P(None, 'gx', 'gy', 'gz'), may hold values from 0 to 2
- affines: float32 [12, 4, 16, 4], P(None, 'gx', 'gy', 'gz'), may hold values from -0.5 to 0.5
- anchor: int32 [1], replicated, may hold values from 0 to 255
Outputs:
- update: float32 [12, 4, 16, 4], P(None, 'gx', 'gy', 'gz')
- residual: float32 [12, 4, 16, 4], P(None, 'gx', 'gy', 'gz')
Inputs may be any that keep to these rules, and one draw needn't show every extreme that they name: `blocks`: number of 256-point correspondence blocks of the correlation; entries of correlations whose second tile lies outside the grid are not read. `anchor`: a tile index (x 16 + y) * 4 + z.
All inputs are finite; a program needn't handle non-finite values.
Results may differ from a plain program's by a relative error of at most 0.0003.
Values sent between devices are 32-bit elements; how exact they have to be, the bound alone decides.
A program may use at most 128 MiB of HBM per device.

v0:
```python
import jax
import jax.numpy as jnp
from jax import lax
from jax.sharding import PartitionSpec as P

BLOCK = 256
ITERS = 10


SPACING = 0.5
DAMPING = 1.0
OFFSETS = (
    (1, 0, 0),
    (0, 1, 0),
    (0, 0, 1),
    (1, 1, -1),
    (1, -1, 1),
    (-1, 1, 1),
    (1, 1, 0),
    (1, 0, 1),
    (0, 1, 1),
    (1, 1, 1),
    (1, -1, 0),
    (0, 1, -1),
    (-1, 0, 1),
)


def padded(value, sides, width):
    for axis, dim in sides:
        devices, length = (lax.axis_size(axis), value.shape[dim])
        up = [(i, (i + 1) % devices) for i in range(devices - 1)]
        down = [(j, i) for i, j in up]
        last = lax.slice_in_dim(value, length - width, length, axis=dim)
        first = lax.slice_in_dim(value, 0, width, axis=dim)
        before = lax.ppermute(last, axis, up)
        after = lax.ppermute(first, axis, down)
        value = jnp.concatenate([before, value, after], axis=dim)
    return value


def spot(offset, rank, first, lengths):
    picks = [slice(None)] * rank
    for axis in range(3):
        picks[first + axis] = slice(1 + offset[axis], 1 + offset[axis] + lengths[axis])
    return tuple(picks)


def window(values, offset, first):
    lengths = tuple((values.shape[first + axis] - 2 for axis in range(3)))
    return values[spot(offset, values.ndim, first, lengths)]


def lifted(points):
    return jnp.concatenate([points, jnp.ones((1,) + points.shape[1:], points.dtype)], axis=0)


def mapped(affine, lifted_points):
    matrix = affine.reshape((3, 4) + affine.shape[1:]) + jnp.eye(3, 4, dtype=affine.dtype).reshape(
        3, 4, 1, 1, 1
    )
    return jnp.einsum("cexyz,exyzp->cxyzp", matrix, lifted_points, precision=lax.Precision.HIGHEST)


def correlation_terms(source, target, normal, weight, affine_here, affine_there, offset):
    exact = lax.Precision.HIGHEST
    source_lift = lifted(source)
    target_lift = lifted(target)
    stride = jnp.asarray(offset, source.dtype).reshape(3, 1, 1, 1, 1) * SPACING
    misfit = jnp.sum(
        normal * (mapped(affine_here, source_lift) - mapped(affine_there, target_lift) - stride),
        axis=0,
    )
    layout = (12,) + source.shape[1:]
    rows_here = (normal[:, None] * source_lift[None]).reshape(layout)
    rows_there = -(normal[:, None] * target_lift[None]).reshape(layout)
    weighted_here = rows_here * weight
    weighted_there = rows_there * weight
    block_here = jnp.einsum("axyzp,bxyzp->abxyz", weighted_here, rows_here, precision=exact)
    block_pair = jnp.einsum("axyzp,bxyzp->abxyz", weighted_here, rows_there, precision=exact)
    block_there = jnp.einsum("axyzp,bxyzp->abxyz", weighted_there, rows_there, precision=exact)
    pull_here = jnp.einsum("axyzp,xyzp->axyz", weighted_here, misfit, precision=exact)
    pull_there = jnp.einsum("axyzp,xyzp->axyz", weighted_there, misfit, precision=exact)
    return (block_here, block_pair, block_there, pull_here, pull_there)


def invert_blocks(blocks):
    left = blocks
    right = jnp.broadcast_to(
        jnp.eye(12, dtype=blocks.dtype).reshape((12, 12) + (1,) * (blocks.ndim - 2)), blocks.shape
    )
    for pivot in range(12):
        factor = 1.0 / left[pivot, pivot]
        row_left = left[pivot] * factor
        row_right = right[pivot] * factor
        column = left[:, pivot]
        left = left - column[:, None] * row_left[None]
        right = right - column[:, None] * row_right[None]
        left = left.at[pivot].set(row_left)
        right = right.at[pivot].set(row_right)
    return right


def fold_back(extended):
    rims = jnp.concatenate([extended[:, :1], extended[:, -1:]], axis=1)
    came = padded(rims, (("gx", 1),), 1)
    inner = extended[:, 1:-1]
    inner = inner.at[:, :1].add(came[:, :1]).at[:, -1:].add(came[:, -1:])
    rims = jnp.concatenate([inner[:, :, :1], inner[:, :, -1:]], axis=2)
    came = padded(rims, (("gy", 2),), 1)
    inner = inner[:, :, 1:-1]
    inner = inner.at[:, :, :1].add(came[:, :, :1]).at[:, :, -1:].add(came[:, :, -1:])
    rims = jnp.concatenate([inner[:, :, :, :1], inner[:, :, :, -1:]], axis=3)
    came = padded(rims, (("gz", 3),), 1)
    inner = inner[:, :, :, 1:-1]
    return inner.at[:, :, :, :1].add(came[:, :, :, :1]).at[:, :, :, -1:].add(came[:, :, :, -1:])


def beside_all(vector):
    return padded(vector, (("gx", 1), ("gy", 2), ("gz", 3)), 1)


def both_products(residual, scaled, image):
    return lax.psum((jnp.sum(residual * scaled), jnp.sum(image * scaled)), ("gx", "gy", "gz"))


def on_device(source_points, target_points, normals, weights, blocks, affines, anchor):
    exact = lax.Precision.HIGHEST
    directions = source_points.shape[1]
    tile_x, tile_y, tile_z = (
        source_points.shape[2],
        source_points.shape[3],
        source_points.shape[4],
    )
    points = source_points.shape[5]
    lengths = (tile_x, tile_y, tile_z)
    span_x = tile_x * lax.axis_size("gx")
    span_y = tile_y * lax.axis_size("gy")
    span_z = tile_z * lax.axis_size("gz")
    wide_x = lax.axis_index("gx") * tile_x - 1 + jnp.arange(tile_x + 2, dtype=jnp.int32)
    wide_y = lax.axis_index("gy") * tile_y - 1 + jnp.arange(tile_y + 2, dtype=jnp.int32)
    wide_z = lax.axis_index("gz") * tile_z - 1 + jnp.arange(tile_z + 2, dtype=jnp.int32)
    inside_x = ((wide_x >= 0) & (wide_x < span_x)).astype(jnp.float32).reshape(-1, 1, 1)
    inside_y = ((wide_y >= 0) & (wide_y < span_y)).astype(jnp.float32).reshape(1, -1, 1)
    inside_z = ((wide_z >= 0) & (wide_z < span_z)).astype(jnp.float32).reshape(1, 1, -1)
    inside_wide = inside_x * inside_y * inside_z
    flat_wide = (
        wide_x.reshape(-1, 1, 1) * span_y + wide_y.reshape(1, -1, 1)
    ) * span_z + wide_z.reshape(1, 1, -1)
    keep_wide = inside_wide * (flat_wide != anchor[0]).astype(jnp.float32)
    keep = keep_wide[1:-1, 1:-1, 1:-1]
    gathered = (
        padded(
            target_points.reshape((3 * directions, tile_x, tile_y, tile_z, points)),
            (("gx", 1), ("gy", 2), ("gz", 3)),
            1,
        ),
        padded(
            affines.reshape((12, tile_x, tile_y, tile_z, 1)), (("gx", 1), ("gy", 2), ("gz", 3)), 1
        ),
    )
    target_wide = gathered[0].reshape((3, directions) + gathered[0].shape[1:])
    affine_wide = gathered[1][..., 0]
    slots = jnp.arange(points, dtype=jnp.int32).reshape(1, 1, 1, points)
    extended = (tile_x + 2, tile_y + 2, tile_z + 2)
    diag = jnp.zeros((12, 12) + lengths, jnp.float32)
    pull = jnp.zeros((12,) + lengths, jnp.float32)
    back_blocks = jnp.zeros((156,) + extended, jnp.float32)
    pairs = []
    for index, offset in enumerate(OFFSETS):
        inside = window(inside_wide, offset, 0)
        live = (slots < BLOCK * blocks[index][..., None]).astype(jnp.float32) * inside[..., None]
        target = window(target_wide[:, index], offset, 1)
        block_here, block_pair, block_there, pull_here, pull_there = correlation_terms(
            source_points[:, index],
            target,
            normals[:, index],
            weights[index] * live,
            affines,
            window(affine_wide, offset, 1),
            offset,
        )
        block_pair = block_pair * (keep * window(keep_wide, offset, 0))
        diag = diag + block_here
        pull = pull + pull_here
        pairs.append(block_pair)
        place = spot(offset, 4, 1, lengths)
        back_blocks = back_blocks.at[place].add(
            jnp.concatenate([block_there.reshape((144,) + lengths), pull_there], axis=0)
        )
    coupling = jnp.stack(pairs)
    folded = fold_back(back_blocks)
    diag = diag + folded[:144].reshape((12, 12) + lengths)
    pull = pull + folded[144:156]
    identity = jnp.eye(12, dtype=jnp.float32).reshape(12, 12, 1, 1, 1)
    diag = keep * (diag + DAMPING * identity) + (1.0 - keep) * identity
    rhs = -(keep * pull)
    inverse = invert_blocks(diag)

    def operate(vector):
        wide = beside_all(vector)
        ahead = jnp.stack([window(wide, offset, 1) for offset in OFFSETS])
        result = jnp.einsum("abxyz,bxyz->axyz", diag, vector, precision=exact)
        result = result + jnp.einsum("dabxyz,dbxyz->axyz", coupling, ahead, precision=exact)
        sent = jnp.einsum("dbaxyz,bxyz->daxyz", coupling, vector, precision=exact)
        back = jnp.zeros((12,) + extended, jnp.float32)
        for index, offset in enumerate(OFFSETS):
            back = back.at[spot(offset, 4, 1, lengths)].add(sent[index])
        return result + fold_back(back)

    def precondition(vector):
        return jnp.einsum("abxyz,bxyz->axyz", inverse, vector, precision=exact)

    update = jnp.zeros_like(rhs)
    residual = rhs
    scaled = precondition(residual)
    image = operate(scaled)
    inner, product = both_products(residual, scaled, image)
    alpha = inner / product
    direction, along = (scaled, image)
    for step in range(ITERS):
        update = update + alpha * direction
        residual = residual - alpha * along
        if step + 1 < ITERS:
            scaled = precondition(residual)
            image = operate(scaled)
            inner_next, product = both_products(residual, scaled, image)
            ratio = inner_next / inner
            alpha = inner_next / (product - ratio * inner_next / alpha)
            direction = scaled + ratio * direction
            along = image + ratio * along
            inner = inner_next
    return (update, residual)


def solution(mesh):
    placed = (
        P(None, None, "gx", "gy", "gz", None),
        P(None, None, "gx", "gy", "gz", None),
        P(None, None, "gx", "gy", "gz", None),
        P(None, "gx", "gy", "gz", None),
        P(None, "gx", "gy", "gz"),
        P(None, "gx", "gy", "gz"),
        P(),
    )
    return jax.shard_map(
        on_device,
        mesh=mesh,
        in_specs=placed,
        out_specs=(P(None, "gx", "gy", "gz"), P(None, "gx", "gy", "gz")),
        check_vma=False,
    )
```

profile of v0, /device:TPU:15, one launch (start us, length us, event | category | flops | bytes accessed | tf_op | source)
XLA Modules:
  0.0 1298.7 jit_solution(10599703377848781927)
XLA Ops:
  123.8 6.5 collective-permute-start.5
  161.5 5.6 pad_maximum_fusion
  198.6 11.4 fusion.203
  355.5 5.7 fusion.452
  402.0 40.5 %all-reduce.46 = (f32[]{:T(128)}, f32[]{:T(128)}) all-reduce(f32[]{:T(128)} %get-tuple-element.2981, f32[]{:T(128)} %get-tuple-element.2980), channel_id=1, replica_groups=mesh['gx'=4,'gy'=4,'gz'=2] {'gx','gy','gz'}, use_global_device_ids=true, to_apply=%region_14.0 | all-reduce | flops 2 | bytes 16 | tf_op jit(solution)/shard_map/psum | solution.py:124
  449.9 5.7 fusion.446
  473.2 5.3 collective-permute-start.34
  494.5 40.4 %all-reduce.45 = (f32[]{:T(128)}, f32[]{:T(128)}) all-reduce(f32[]{:T(128)} %get-tuple-element.2979, f32[]{:T(128)} %get-tuple-element.2978), channel_id=1, replica_groups=mesh['gx'=4,'gy'=4,'gz'=2] {'gx','gy','gz'}, use_global_device_ids=true, to_apply=%region_18.0 | all-reduce | flops 2 | bytes 16 | tf_op jit(solution)/shard_map/psum | solution.py:124
  545.4 5.7 fusion.440
  568.7 5.3 collective-permute-start.46
  589.6 40.5 %all-reduce.44 = (f32[]{:T(128)}, f32[]{:T(128)}) all-reduce(f32[]{:T(128)} %get-tuple-element.2977, f32[]{:T(128)} %get-tuple-element.2976), channel_id=1, replica_groups=mesh['gx'=4,'gy'=4,'gz'=2] {'gx','gy','gz'}, use_global_device_ids=true, to_apply=%region_22.0 | all-reduce | flops 2 | bytes 16 | tf_op jit(solution)/shard_map/psum | solution.py:124
  640.1 5.7 fusion.434
  663.4 5.3 collective-permute-start.58
  684.8 40.5 %all-reduce.43 = (f32[]{:T(128)}, f32[]{:T(128)}) all-reduce(f32[]{:T(128)} %get-tuple-element.2975, f32[]{:T(128)} %get-tuple-element.2974), channel_id=1, replica_groups=mesh['gx'=4,'gy'=4,'gz'=2] {'gx','gy','gz'}, use_global_device_ids=true, to_apply=%region_26.0 | all-reduce | flops 2 | bytes 16 | tf_op jit(solution)/shard_map/psum | solution.py:124
  735.1 5.7 fusion.428
  758.4 5.3 collective-permute-start.70
  779.3 40.5 %all-reduce.42 = (f32[]{:T(128)}, f32[]{:T(128)}) all-reduce(f32[]{:T(128)} %get-tuple-element.2973, f32[]{:T(128)} %get-tuple-element.2972), channel_id=1, replica_groups=mesh['gx'=4,'gy'=4,'gz'=2] {'gx','gy','gz'}, use_global_device_ids=true, to_apply=%region_30.0 | all-reduce | flops 2 | bytes 16 | tf_op jit(solution)/shard_map/psum | solution.py:124
  829.7 5.7 fusion.422
  853.0 5.3 collective-permute-start.82
  874.2 40.5 %all-reduce.41 = (f32[]{:T(128)}, f32[]{:T(128)}) all-reduce(f32[]{:T(128)} %get-tuple-element.2971, f32[]{:T(128)} %get-tuple-element.2970), channel_id=1, replica_groups=mesh['gx'=4,'gy'=4,'gz'=2] {'gx','gy','gz'}, use_global_device_ids=true, to_apply=%region_34.0 | all-reduce | flops 2 | bytes 16 | tf_op jit(solution)/shard_map/psum | solution.py:124
  924.5 5.7 fusion.416
  947.8 5.3 collective-permute-start.94
  968.8 40.5 %all-reduce.40 = (f32[]{:T(128)}, f32[]{:T(128)}) all-reduce(f32[]{:T(128)} %get-tuple-element.2969, f32[]{:T(128)} %get-tuple-element.2968), channel_id=1, replica_groups=mesh['gx'=4,'gy'=4,'gz'=2] {'gx','gy','gz'}, use_global_device_ids=true, to_apply=%region_38.0 | all-reduce | flops 2 | bytes 16 | tf_op jit(solution)/shard_map/psum | solution.py:124
  1019.1 5.7 fusion.410
  1042.4 5.3 collective-permute-start.106
  1063.7 40.5 %all-reduce.39 = (f32[]{:T(128)}, f32[]{:T(128)}) all-reduce(f32[]{:T(128)} %get-tuple-element.2967, f32[]{:T(128)} %get-tuple-element.2966), channel_id=1, replica_groups=mesh['gx'=4,'gy'=4,'gz'=2] {'gx','gy','gz'}, use_global_device_ids=true, to_apply=%region_42.0 | all-reduce | flops 2 | bytes 16 | tf_op jit(solution)/shard_map/psum | solution.py:124
  1114.0 5.7 fusion.404
  1137.3 5.3 collective-permute-start.118
  1158.2 40.5 %all-reduce.38 = (f32[]{:T(128)}, f32[]{:T(128)}) all-reduce(f32[]{:T(128)} %get-tuple-element.2965, f32[]{:T(128)} %get-tuple-element.2964), channel_id=1, replica_groups=mesh['gx'=4,'gy'=4,'gz'=2] {'gx','gy','gz'}, use_global_device_ids=true, to_apply=%region_46.0 | all-reduce | flops 2 | bytes 16 | tf_op jit(solution)/shard_map/psum | solution.py:124
  1208.6 5.7 fusion.398
  1231.9 5.3 collective-permute-start.130
  1252.9 40.5 %all-reduce.37 = (f32[]{:T(128)}, f32[]{:T(128)}) all-reduce(f32[]{:T(128)} %get-tuple-element.2963, f32[]{:T(128)} %get-tuple-element.2962), channel_id=1, replica_groups=mesh['gx'=4,'gy'=4,'gz'=2] {'gx','gy','gz'}, use_global_device_ids=true, to_apply=%region_50.0 | all-reduce | flops 2 | bytes 16 | tf_op jit(solution)/shard_map/psum | solution.py:124
  (1706 shorter events, 720.0 us)
Async XLA Ops:
  0.6 50.2 %collective-permute-start = (f32[39,1,4,2,512]{4,3,2,1,0:T(2,128)}, f32[39,1,4,2,512]{4,3,2,1,0:T(2,128)S(1)}, u32[]{:S(2)}, u32[]{:S(2)}) collective-permute-start(f32[39,1,4,2,512]{4,3,2,1,0:T(2,128)} %bitcast.2152), channel_id=1, source_target_pairs={{0,8},{8,16},{16,24},{1,9},{9,17},{17,25},{2,10},{10,18},{18,26},{... | collective-permute-start | bytes 1916936 | tf_op jit(solution)/shard_map/ppermute | solution.py:36
  4.0 46.9 %collective-permute-start.1 = (f32[39,1,4,2,512]{4,3,2,1,0:T(2,128)}, f32[39,1,4,2,512]{4,3,2,1,0:T(2,128)S(1)}, u32[]{:S(2)}, u32[]{:S(2)}) collective-permute-start(f32[39,1,4,2,512]{4,3,2,1,0:T(2,128)} %bitcast.2153), channel_id=1, source_target_pairs={{8,0},{16,8},{24,16},{9,1},{17,9},{25,17},{10,2},{18,10},{26,18},{... | collective-permute-start | bytes 1916936 | tf_op jit(solution)/shard_map/ppermute | solution.py:37
  6.8 127.8 %collective-permute-start.6 = (f32[12,1,4,2,1]{0,2,4,3,1:T(4,128)S(1)}, f32[12,1,4,2,1]{0,2,4,3,1:T(4,128)}, u32[]{:S(2)}, u32[]{:S(2)}) collective-permute-start(f32[12,1,4,2,1]{0,2,4,3,1:T(4,128)S(1)} %bitcast.2434), channel_id=1, source_target_pairs={{0,8},{8,16},{16,24},{1,9},{9,17},{17,25},{2,10},{10,18},{18,26},{... | collective-permute-start | bytes 1160 | tf_op jit(solution)/shard_map/ppermute | solution.py:36
  10.0 124.6 %collective-permute-start.7 = (f32[12,1,4,2,1]{0,2,4,3,1:T(4,128)S(1)}, f32[12,1,4,2,1]{0,2,4,3,1:T(4,128)}, u32[]{:S(2)}, u32[]{:S(2)}) collective-permute-start(f32[12,1,4,2,1]{0,2,4,3,1:T(4,128)S(1)} %bitcast.2435), channel_id=1, source_target_pairs={{8,0},{16,8},{24,16},{9,1},{17,9},{25,17},{10,2},{18,10},{26,18},{... | collective-permute-start | bytes 1160 | tf_op jit(solution)/shard_map/ppermute | solution.py:37
  52.2 64.7 %collective-permute-start.2 = (f32[39,3,1,2,512]{4,3,2,1,0:T(2,128)}, f32[39,3,1,2,512]{4,3,2,1,0:T(2,128)S(1)}, u32[]{:S(2)}, u32[]{:S(2)}) collective-permute-start(f32[39,3,1,2,512]{4,3,2,1,0:T(2,128)} %get-tuple-element.3030), channel_id=1, source_target_pairs={{0,2},{2,4},{4,6},{1,3},{3,5},{5,7},{8,10},{10,12},{12,14},{9,11},... | collective-permute-start | bytes 1437704 | tf_op jit(solution)/shard_map/ppermute | solution.py:36
  53.6 63.4 %collective-permute-start.3 = (f32[39,3,1,2,512]{4,3,2,1,0:T(2,128)}, f32[39,3,1,2,512]{4,3,2,1,0:T(2,128)S(1)}, u32[]{:S(2)}, u32[]{:S(2)}) collective-permute-start(f32[39,3,1,2,512]{4,3,2,1,0:T(2,128)} %get-tuple-element.3031), channel_id=1, source_target_pairs={{2,0},{4,2},{6,4},{3,1},{5,3},{7,5},{10,8},{12,10},{14,12},{11,9},... | collective-permute-start | bytes 1437704 | tf_op jit(solution)/shard_map/ppermute | solution.py:37
  122.5 39.0 %collective-permute-start.4 = (f32[39,3,6,1,512]{4,3,2,1,0:T(1,128)}, f32[39,3,6,1,512]{4,3,2,1,0:T(1,128)}, u32[]{:S(2)}, u32[]{:S(2)}) collective-permute-start(f32[39,3,6,1,512]{4,3,2,1,0:T(1,128)} %get-tuple-element.3028), channel_id=1, source_target_pairs={{0,1},{2,3},{4,5},{6,7},{8,9},{10,11},{12,13},{14,15},{16,17},{18,... | collective-permute-start | bytes 4313096 | tf_op jit(solution)/shard_map/ppermute | solution.py:36
  123.8 37.7 %collective-permute-start.5 = (f32[39,3,6,1,512]{4,3,2,1,0:T(1,128)}, f32[39,3,6,1,512]{4,3,2,1,0:T(1,128)}, u32[]{:S(2)}, u32[]{:S(2)}) collective-permute-start(f32[39,3,6,1,512]{4,3,2,1,0:T(1,128)} %get-tuple-element.3029), channel_id=1, source_target_pairs={{1,0},{3,2},{5,4},{7,6},{9,8},{11,10},{13,12},{15,14},{17,16},{19,... | collective-permute-start | bytes 4313096 | tf_op jit(solution)/shard_map/ppermute | solution.py:37
  275.9 50.4 %collective-permute-start.12 = (f32[156,1,6,4]{0,3,2,1:T(4,128)S(1)}, f32[156,1,6,4]{0,3,2,1:T(4,128)S(1)}, u32[]{:S(2)}, u32[]{:S(2)}) collective-permute-start(f32[156,1,6,4]{0,3,2,1:T(4,128)S(1)} %get-tuple-element.3070), channel_id=1, source_target_pairs={{0,8},{8,16},{16,24},{1,9},{9,17},{17,25},{2,10},{10,18},{18,26},{... | collective-permute-start | bytes 44936 | tf_op jit(solution)/shard_map/ppermute | solution.py:36
  278.5 47.8 %collective-permute-start.13 = (f32[156,1,6,4]{0,3,2,1:T(4,128)S(1)}, f32[156,1,6,4]{0,3,2,1:T(4,128)S(1)}, u32[]{:S(2)}, u32[]{:S(2)}) collective-permute-start(f32[156,1,6,4]{0,3,2,1:T(4,128)S(1)} %get-tuple-element.3071), channel_id=1, source_target_pairs={{8,0},{16,8},{24,16},{9,1},{17,9},{25,17},{10,2},{18,10},{26,18},{... | collective-permute-start | bytes 44936 | tf_op jit(solution)/shard_map/ppermute | solution.py:37
  349.9 21.2 %collective-permute-start.18 = (f32[12,1,4,2]{0,3,2,1:T(2,128)S(1)}, f32[12,1,4,2]{0,3,2,1:T(2,128)S(1)}, u32[]{:S(2)}, u32[]{:S(2)}) collective-permute-start(f32[12,1,4,2]{0,3,2,1:T(2,128)S(1)} %bitcast.2227), channel_id=1, source_target_pairs={{8,0},{16,8},{24,16},{9,1},{17,9},{25,17},{10,2},{18,10},{26,18},{... | collective-permute-start | bytes 1160 | tf_op jit(solution)/shard_map/ppermute | solution.py:37
  365.7 21.3 %collective-permute-start.24 = (f32[12,1,6,4]{0,3,2,1:T(4,128)S(1)}, f32[12,1,6,4]{0,3,2,1:T(4,128)S(1)}, u32[]{:S(2)}, u32[]{:S(2)}) collective-permute-start(f32[12,1,6,4]{0,3,2,1:T(4,128)S(1)} %get-tuple-element.3259), channel_id=1, source_target_pairs={{0,8},{8,16},{16,24},{1,9},{9,17},{17,25},{2,10},{10,18},{18,26},{... | collective-permute-start | bytes 3464 | tf_op jit(solution)/shard_map/ppermute | solution.py:36
  444.1 21.3 %collective-permute-start.30 = (f32[12,1,4,2]{0,3,2,1:T(2,128)S(1)}, f32[12,1,4,2]{0,3,2,1:T(2,128)S(1)}, u32[]{:S(2)}, u32[]{:S(2)}) collective-permute-start(f32[12,1,4,2]{0,3,2,1:T(2,128)S(1)} %bitcast.2238), channel_id=1, source_target_pairs={{8,0},{16,8},{24,16},{9,1},{17,9},{25,17},{10,2},{18,10},{26,18},{... | collective-permute-start | bytes 1160 | tf_op jit(solution)/shard_map/ppermute | solution.py:37
  460.0 19.8 %collective-permute-start.36 = (f32[12,1,6,4]{0,3,2,1:T(4,128)S(1)}, f32[12,1,6,4]{0,3,2,1:T(4,128)S(1)}, u32[]{:S(2)}, u32[]{:S(2)}) collective-permute-start(f32[12,1,6,4]{0,3,2,1:T(4,128)S(1)} %get-tuple-element.3257), channel_id=1, source_target_pairs={{0,8},{8,16},{16,24},{1,9},{9,17},{17,25},{2,10},{10,18},{18,26},{... | collective-permute-start | bytes 3464 | tf_op jit(solution)/shard_map/ppermute | solution.py:36
  473.2 19.4 %collective-permute-start.34 = (f32[12,3,6,1]{0,3,2,1:T(1,128)S(1)}, f32[12,3,6,1]{0,3,2,1:T(1,128)S(1)}, u32[]{:S(2)}, u32[]{:S(2)}) collective-permute-start(f32[12,3,6,1]{0,3,2,1:T(1,128)S(1)} %get-tuple-element.3371), channel_id=1, source_target_pairs={{1,0},{3,2},{5,4},{7,6},{9,8},{11,10},{13,12},{15,14},{17,16},{19,... | collective-permute-start | bytes 2600 | tf_op jit(solution)/shard_map/ppermute | solution.py:37
  539.5 21.3 %collective-permute-start.42 = (f32[12,1,4,2]{0,3,2,1:T(2,128)S(1)}, f32[12,1,4,2]{0,3,2,1:T(2,128)S(1)}, u32[]{:S(2)}, u32[]{:S(2)}) collective-permute-start(f32[12,1,4,2]{0,3,2,1:T(2,128)S(1)} %bitcast.2249), channel_id=1, source_target_pairs={{8,0},{16,8},{24,16},{9,1},{17,9},{25,17},{10,2},{18,10},{26,18},{... | collective-permute-start | bytes 1160 | tf_op jit(solution)/shard_map/ppermute | solution.py:37
  555.5 19.8 %collective-permute-start.48 = (f32[12,1,6,4]{0,3,2,1:T(4,128)S(1)}, f32[12,1,6,4]{0,3,2,1:T(4,128)S(1)}, u32[]{:S(2)}, u32[]{:S(2)}) collective-permute-start(f32[12,1,6,4]{0,3,2,1:T(4,128)S(1)} %get-tuple-element.3255), channel_id=1, source_target_pairs={{0,8},{8,16},{16,24},{1,9},{9,17},{17,25},{2,10},{10,18},{18,26},{... | collective-permute-start | bytes 3464 | tf_op jit(solution)/shard_map/ppermute | solution.py:36
  634.2 21.3 %collective-permute-start.54 = (f32[12,1,4,2]{0,3,2,1:T(2,128)S(1)}, f32[12,1,4,2]{0,3,2,1:T(2,128)S(1)}, u32[]{:S(2)}, u32[]{:S(2)}) collective-permute-start(f32[12,1,4,2]{0,3,2,1:T(2,128)S(1)} %bitcast.2260), channel_id=1, source_target_pairs={{8,0},{16,8},{24,16},{9,1},{17,9},{25,17},{10,2},{18,10},{26,18},{... | collective-permute-start | bytes 1160 | tf_op jit(solution)/shard_map/ppermute | solution.py:37
  650.2 19.8 %collective-permute-start.60 = (f32[12,1,6,4]{0,3,2,1:T(4,128)S(1)}, f32[12,1,6,4]{0,3,2,1:T(4,128)S(1)}, u32[]{:S(2)}, u32[]{:S(2)}) collective-permute-start(f32[12,1,6,4]{0,3,2,1:T(4,128)S(1)} %get-tuple-element.3253), channel_id=1, source_target_pairs={{0,8},{8,16},{16,24},{1,9},{9,17},{17,25},{2,10},{10,18},{18,26},{... | collective-permute-start | bytes 3464 | tf_op jit(solution)/shard_map/ppermute | solution.py:36
  663.4 19.6 %collective-permute-start.58 = (f32[12,3,6,1]{0,3,2,1:T(1,128)S(1)}, f32[12,3,6,1]{0,3,2,1:T(1,128)S(1)}, u32[]{:S(2)}, u32[]{:S(2)}) collective-permute-start(f32[12,3,6,1]{0,3,2,1:T(1,128)S(1)} %get-tuple-element.3365), channel_id=1, source_target_pairs={{1,0},{3,2},{5,4},{7,6},{9,8},{11,10},{13,12},{15,14},{17,16},{19,... | collective-permute-start | bytes 2600 | tf_op jit(solution)/shard_map/ppermute | solution.py:37
  729.2 21.3 %collective-permute-start.66 = (f32[12,1,4,2]{0,3,2,1:T(2,128)S(1)}, f32[12,1,4,2]{0,3,2,1:T(2,128)S(1)}, u32[]{:S(2)}, u32[]{:S(2)}) collective-permute-start(f32[12,1,4,2]{0,3,2,1:T(2,128)S(1)} %bitcast.2271), channel_id=1, source_target_pairs={{8,0},{16,8},{24,16},{9,1},{17,9},{25,17},{10,2},{18,10},{26,18},{... | collective-permute-start | bytes 1160 | tf_op jit(solution)/shard_map/ppermute | solution.py:37
  745.2 19.8 %collective-permute-start.72 = (f32[12,1,6,4]{0,3,2,1:T(4,128)S(1)}, f32[12,1,6,4]{0,3,2,1:T(4,128)S(1)}, u32[]{:S(2)}, u32[]{:S(2)}) collective-permute-start(f32[12,1,6,4]{0,3,2,1:T(4,128)S(1)} %get-tuple-element.3251), channel_id=1, source_target_pairs={{0,8},{8,16},{16,24},{1,9},{9,17},{17,25},{2,10},{10,18},{18,26},{... | collective-permute-start | bytes 3464 | tf_op jit(solution)/shard_map/ppermute | solution.py:36
  823.9 21.3 %collective-permute-start.78 = (f32[12,1,4,2]{0,3,2,1:T(2,128)S(1)}, f32[12,1,4,2]{0,3,2,1:T(2,128)S(1)}, u32[]{:S(2)}, u32[]{:S(2)}) collective-permute-start(f32[12,1,4,2]{0,3,2,1:T(2,128)S(1)} %bitcast.2282), channel_id=1, source_target_pairs={{8,0},{16,8},{24,16},{9,1},{17,9},{25,17},{10,2},{18,10},{26,18},{... | collective-permute-start | bytes 1160 | tf_op jit(solution)/shard_map/ppermute | solution.py:37
  839.8 19.8 %collective-permute-start.84 = (f32[12,1,6,4]{0,3,2,1:T(4,128)S(1)}, f32[12,1,6,4]{0,3,2,1:T(4,128)S(1)}, u32[]{:S(2)}, u32[]{:S(2)}) collective-permute-start(f32[12,1,6,4]{0,3,2,1:T(4,128)S(1)} %get-tuple-element.3249), channel_id=1, source_target_pairs={{0,8},{8,16},{16,24},{1,9},{9,17},{17,25},{2,10},{10,18},{18,26},{... | collective-permute-start | bytes 3464 | tf_op jit(solution)/shard_map/ppermute | solution.py:36
  918.7 21.3 %collective-permute-start.90 = (f32[12,1,4,2]{0,3,2,1:T(2,128)S(1)}, f32[12,1,4,2]{0,3,2,1:T(2,128)S(1)}, u32[]{:S(2)}, u32[]{:S(2)}) collective-permute-start(f32[12,1,4,2]{0,3,2,1:T(2,128)S(1)} %bitcast.2293), channel_id=1, source_target_pairs={{8,0},{16,8},{24,16},{9,1},{17,9},{25,17},{10,2},{18,10},{26,18},{... | collective-permute-start | bytes 1160 | tf_op jit(solution)/shard_map/ppermute | solution.py:37
  934.6 19.8 %collective-permute-start.96 = (f32[12,1,6,4]{0,3,2,1:T(4,128)S(1)}, f32[12,1,6,4]{0,3,2,1:T(4,128)S(1)}, u32[]{:S(2)}, u32[]{:S(2)}) collective-permute-start(f32[12,1,6,4]{0,3,2,1:T(4,128)S(1)} %get-tuple-element.3247), channel_id=1, source_target_pairs={{0,8},{8,16},{16,24},{1,9},{9,17},{17,25},{2,10},{10,18},{18,26},{... | collective-permute-start | bytes 3464 | tf_op jit(solution)/shard_map/ppermute | solution.py:36
  1013.3 21.3 %collective-permute-start.102 = (f32[12,1,4,2]{0,3,2,1:T(2,128)S(1)}, f32[12,1,4,2]{0,3,2,1:T(2,128)S(1)}, u32[]{:S(2)}, u32[]{:S(2)}) collective-permute-start(f32[12,1,4,2]{0,3,2,1:T(2,128)S(1)} %bitcast.2304), channel_id=1, source_target_pairs={{8,0},{16,8},{24,16},{9,1},{17,9},{25,17},{10,2},{18,10},{26,18},{... | collective-permute-start | bytes 1160 | tf_op jit(solution)/shard_map/ppermute | solution.py:37
  1029.2 19.8 %collective-permute-start.108 = (f32[12,1,6,4]{0,3,2,1:T(4,128)S(1)}, f32[12,1,6,4]{0,3,2,1:T(4,128)S(1)}, u32[]{:S(2)}, u32[]{:S(2)}) collective-permute-start(f32[12,1,6,4]{0,3,2,1:T(4,128)S(1)} %get-tuple-element.3245), channel_id=1, source_target_pairs={{0,8},{8,16},{16,24},{1,9},{9,17},{17,25},{2,10},{10,18},{18,26},{... | collective-permute-start | bytes 3464 | tf_op jit(solution)/shard_map/ppermute | solution.py:36
  1108.1 21.3 %collective-permute-start.114 = (f32[12,1,4,2]{0,3,2,1:T(2,128)S(1)}, f32[12,1,4,2]{0,3,2,1:T(2,128)S(1)}, u32[]{:S(2)}, u32[]{:S(2)}) collective-permute-start(f32[12,1,4,2]{0,3,2,1:T(2,128)S(1)} %bitcast.2315), channel_id=1, source_target_pairs={{8,0},{16,8},{24,16},{9,1},{17,9},{25,17},{10,2},{18,10},{26,18},{... | collective-permute-start | bytes 1160 | tf_op jit(solution)/shard_map/ppermute | solution.py:37
  1124.1 19.8 %collective-permute-start.120 = (f32[12,1,6,4]{0,3,2,1:T(4,128)S(1)}, f32[12,1,6,4]{0,3,2,1:T(4,128)S(1)}, u32[]{:S(2)}, u32[]{:S(2)}) collective-permute-start(f32[12,1,6,4]{0,3,2,1:T(4,128)S(1)} %get-tuple-element.3243), channel_id=1, source_target_pairs={{0,8},{8,16},{16,24},{1,9},{9,17},{17,25},{2,10},{10,18},{18,26},{... | collective-permute-start | bytes 3464 | tf_op jit(solution)/shard_map/ppermute | solution.py:36
  1202.7 21.3 %collective-permute-start.126 = (f32[12,1,4,2]{0,3,2,1:T(2,128)S(1)}, f32[12,1,4,2]{0,3,2,1:T(2,128)S(1)}, u32[]{:S(2)}, u32[]{:S(2)}) collective-permute-start(f32[12,1,4,2]{0,3,2,1:T(2,128)S(1)} %bitcast.2326), channel_id=1, source_target_pairs={{8,0},{16,8},{24,16},{9,1},{17,9},{25,17},{10,2},{18,10},{26,18},{... | collective-permute-start | bytes 1160 | tf_op jit(solution)/shard_map/ppermute | solution.py:37
  1218.7 19.8 %collective-permute-start.132 = (f32[12,1,6,4]{0,3,2,1:T(4,128)S(1)}, f32[12,1,6,4]{0,3,2,1:T(4,128)S(1)}, u32[]{:S(2)}, u32[]{:S(2)}) collective-permute-start(f32[12,1,6,4]{0,3,2,1:T(4,128)S(1)} %get-tuple-element.3241), channel_id=1, source_target_pairs={{0,8},{8,16},{16,24},{1,9},{9,17},{17,25},{2,10},{10,18},{18,26},{... | collective-permute-start | bytes 3464 | tf_op jit(solution)/shard_map/ppermute | solution.py:36
  (293 other events, 3054.7 us)
where the time goes:
time: 1320 us; the launch traced here: 1300 us
  blocking collectives  405 us (31%)
  starting transfers between devices  382 us (29%)
  local copies, waits for them, and re-layouts  174 us (13%)
  matrix products  170 us (13%)
  other arithmetic  75 us (6%)
  waiting for transfers between devices  47.6 us (4%)
  between operations  46.2 us (4%)
    psum x10, blocking collectives, both_products(): lax.psum((jnp.sum(residual * scaled), jnp.sum(image * scaled)), ('gx', 'g...  405 us
    ppermute x69, starting transfers between devices, padded(): after = lax.ppermute(first, axis, down)  267 us
    ppermute x69, starting transfers between devices, padded(): before = lax.ppermute(last, axis, up)  114 us
    dot_general x10, matrix products, operate(): sent = jnp.einsum('dbaxyz,bxyz->daxyz', coupling, vector, precision=exact)  56.8 us
    ppermute x69, waiting for transfers between devices, padded(): before = lax.ppermute(last, axis, up)  31.7 us
    another operation x65, local copies, waits for them, and re-layouts  28.1 us
  transfers between devices with their start and end apart: 138, of which 32 were waited for; matrix products, arithmetic and copies ran while one was open for 22% of the time, Pallas kernels for 0%

commit v1 on v0

v1 whole, which is shorter than its diff:
```python
import functools

import jax
import jax.numpy as jnp
import numpy as np
from jax import lax
from jax.experimental import pallas as pl
from jax.experimental.pallas import tpu as pltpu
from jax.sharding import PartitionSpec as P

BLOCK = 256
ITERS = 10
SPACING = 0.5
DAMPING = 1.0
OFFSETS = (
    (1, 0, 0),
    (0, 1, 0),
    (0, 0, 1),
    (1, 1, -1),
    (1, -1, 1),
    (-1, 1, 1),
    (1, 1, 0),
    (1, 0, 1),
    (0, 1, 1),
    (1, 1, 1),
    (1, -1, 0),
    (0, 1, -1),
    (-1, 0, 1),
)
DIRS = len(OFFSETS)
SLOTS = 16
PAIR_ROWS = 96
BACK_ROWS = 64
ROWS = PAIR_ROWS + BACK_ROWS
AXES = ("gx", "gy", "gz")
MESH = pl.DeviceIdType.MESH
VMEM_BYTES = 60 * 1024 * 1024

NORMAL_PAIRS = [(c, k) for c in range(3) for k in range(c, 3)]
POINT_PAIRS = [(e, k) for e in range(4) for k in range(e, 4)]


def normal_pair(c, k):
    return NORMAL_PAIRS.index((min(c, k), max(c, k)))


def point_pair(e, k):
    return POINT_PAIRS.index((min(e, k), max(e, k)))


def moved_targets(target):
    views = {d: target[:, d] for d in range(DIRS)}
    for axis, name in enumerate(AXES):
        dim = 1 + axis
        devices = lax.axis_size(name)
        for sign in (1, -1):
            members = [d for d in range(DIRS) if OFFSETS[d][axis] == sign]
            if not members:
                continue
            length = views[members[0]].shape[dim]
            edge = 0 if sign > 0 else length - 1
            slab = jnp.stack(
                [lax.slice_in_dim(views[d], edge, edge + 1, axis=dim) for d in members]
            )
            if sign > 0:
                links = [(i + 1, i) for i in range(devices - 1)]
            else:
                links = [(i, i + 1) for i in range(devices - 1)]
            came = lax.ppermute(slab, name, links)
            for place, d in enumerate(members):
                if sign > 0:
                    kept = lax.slice_in_dim(views[d], 1, length, axis=dim)
                    pieces = [kept, came[place]]
                else:
                    kept = lax.slice_in_dim(views[d], 0, length - 1, axis=dim)
                    pieces = [came[place], kept]
                views[d] = jnp.concatenate(pieces, axis=dim)
    return jnp.stack([views[d] for d in range(DIRS)], axis=1)


def assemble_kernel(tiles, source, target, normal, weight, lane_table, affine, out, turned, acc):
    width = source.shape[1]
    points = source.shape[2]
    for start in range(0, points, 128):
        spots = pl.ds(start, 128)
        for c in range(3):
            turned[c, spots, :] = source[c, :, spots].T
            turned[3 + c, spots, :] = target[c, :, spots].T
            turned[6 + c, spots, :] = normal[c, :, spots].T
        turned[9, spots, :] = weight[:, spots].T
    acc[...] = jnp.zeros_like(acc)
    step = 32
    limit = lane_table[3:4, :]

    def body(chunk, carry):
        base = pl.multiple_of(chunk * step, step)
        spots = pl.ds(base, step)
        p = [turned[c, spots, :] for c in range(3)] + [None]
        q = [turned[3 + c, spots, :] for c in range(3)] + [None]
        n = [turned[6 + c, spots, :] for c in range(3)]
        index = base + lax.broadcasted_iota(jnp.int32, (step, width), 0)
        w = jnp.where(index.astype(jnp.float32) < limit, turned[9, spots, :], 0.0)

        def times(left, right):
            if left is None:
                return right
            return left if right is None else left * right

        def add(row, value):
            acc[row] += jnp.sum(value.reshape(step // 8, 8, width), axis=0)

        weighted = [w * n[c] * n[k] for c, k in NORMAL_PAIRS]
        for e in range(4):
            for k in range(4):
                product = times(p[e], q[k])
                for s in range(6):
                    add(s * 16 + e * 4 + k, times(weighted[s], product))
        for first, here in ((PAIR_ROWS, q), (ROWS, p)):
            for place, (e, k) in enumerate(POINT_PAIRS):
                product = times(here[e], here[k])
                for s in range(6):
                    add(first + s * 10 + place, times(weighted[s], product))
        return carry

    lax.fori_loop(0, points // step, body, 0)

    lane = lax.broadcasted_iota(jnp.int32, (8, width), 1)
    in_pairs = lane < DIRS * tiles

    def all_slots(value):
        for span in (8, 4, 2, 1):
            value = value + pltpu.roll(value, span * tiles, 1)
        return value

    here_rows = [jnp.sum(acc[ROWS + r : ROWS + r + 8], axis=1) for r in range(0, BACK_ROWS, 8)]
    stride = []
    for c in range(3):
        for e in range(4):
            total = 0.0
            for k in range(3):
                row = normal_pair(c, k) * 10 + point_pair(e, 3)
                total = total + here_rows[row // 8][row % 8 : row % 8 + 1] * lane_table[k : k + 1, :]
            stride.append(total)
    stride += [jnp.zeros((1, width), jnp.float32)] * 4
    last_slot = lane >= (SLOTS - 1) * tiles
    for r in range(0, PAIR_ROWS, 8):
        rows = jnp.sum(acc[r : r + 8], axis=1)
        if r < 16:
            rows = rows + affine[r : r + 8, :]
            rows = jnp.where(last_slot, all_slots(jnp.concatenate(stride[r : r + 8], axis=0)), rows)
        out[r : r + 8, :] = rows
    for r in range(0, BACK_ROWS, 8):
        there = jnp.sum(acc[PAIR_ROWS + r : PAIR_ROWS + r + 8], axis=1)
        out[PAIR_ROWS + r : PAIR_ROWS + r + 8, :] = jnp.where(
            in_pairs, there, all_slots(here_rows[r // 8])
        )


def gather_kernel(sizes, mine, out, local_sem, send_sem, recv_sem, hand_sem, take_sem):
    count_x, count_y, count_z = sizes
    chips_z = count_z // 2
    chips = count_x * count_y * chips_z
    at_x, at_y, at_z = (lax.axis_index(name) for name in AXES)
    core = at_z % 2
    chip = (at_x * count_y + at_y) * chips_z + at_z // 2

    def place(which, on_core):
        z = (which % chips_z) * 2 + on_core
        rest = which // chips_z
        return rest // count_y, rest % count_y, z

    def slot(which, on_core):
        x, y, z = place(which, on_core)
        return (x * count_y + y) * count_z + z

    barrier = pltpu.get_barrier_semaphore()
    sibling = place(chip, 1 - core)

    def greet(k, carry):
        other = place((chip + k) % chips, core)
        pl.semaphore_signal(barrier, inc=1, device_id=other, device_id_type=MESH)
        return carry

    lax.fori_loop(1, chips, greet, 0)
    pl.semaphore_signal(barrier, inc=1, device_id=sibling, device_id_type=MESH)
    pl.semaphore_wait(barrier, chips)

    me = slot(chip, core)
    own = pltpu.make_async_copy(mine, out.at[me], local_sem)
    own.start()

    def outgoing(k):
        return pltpu.make_async_remote_copy(
            src_ref=mine,
            dst_ref=out.at[me],
            send_sem=send_sem.at[k],
            recv_sem=recv_sem.at[k],
            device_id=place((chip + k) % chips, core),
            device_id_type=MESH,
        )

    def handed(k):
        origin = slot((chip + chips - k) % chips, core)
        return pltpu.make_async_remote_copy(
            src_ref=out.at[origin],
            dst_ref=out.at[origin],
            send_sem=hand_sem.at[k],
            recv_sem=take_sem.at[k],
            device_id=sibling,
            device_id_type=MESH,
        )

    def first_hand():
        return pltpu.make_async_remote_copy(
            src_ref=mine,
            dst_ref=out.at[me],
            send_sem=hand_sem.at[0],
            recv_sem=take_sem.at[0],
            device_id=sibling,
            device_id_type=MESH,
        )

    def send(k, carry):
        outgoing(k).start()
        return carry

    def forward(k, carry):
        outgoing(k).wait_recv()
        handed(k).start()
        return carry

    def finish(k, carry):
        outgoing(k).wait_send()
        handed(k).wait()
        return carry

    lax.fori_loop(1, chips, send, 0)
    first_hand().start()
    lax.fori_loop(1, chips, forward, 0)
    first_hand().wait()
    lax.fori_loop(1, chips, finish, 0)
    own.wait()


def turn_kernel(tiles, gathered, out):
    width = gathered.shape[2]

    def body(chunk, carry):
        rows = pl.ds(pl.multiple_of(chunk * 8, 8), 8)
        slot = lax.broadcasted_iota(jnp.int32, (8, width), 1) // tiles
        values = [gathered[j, rows, :] for j in range(SLOTS)]
        for span in (1, 2, 4, 8):
            low = (slot & span) == 0
            fresh = list(values)
            for j in range(SLOTS):
                if j & span:
                    continue
                first, second = values[j], values[j + span]
                fresh[j] = jnp.where(low, first, pltpu.roll(second, span * tiles, 1))
                fresh[j + span] = jnp.where(
                    low, pltpu.roll(first, width - span * tiles, 1), second
                )
            values = fresh
        for j in range(SLOTS):
            out[j, rows, :] = values[j]
        return carry

    lax.fori_loop(0, ROWS // 8, body, 0)


def solve_kernel(
    bricks, devices, anchor, parts, table, update_out, residual_out, blocks, inverse, ahead, sent, image
):
    span = parts.shape[2]
    tiles = bricks[0] * bricks[1] * bricks[2]
    inner = (bricks[1] * bricks[2], bricks[2], 1)
    outer = (devices[1] * devices[2] * tiles, devices[2] * tiles, tiles)

    def pull(value, axis, sign):
        near = (sign * inner[axis]) % span
        far = (sign * (outer[axis] - (bricks[axis] - 1) * inner[axis])) % span
        row = axis * 4 + (0 if sign > 0 else 2)
        result = pltpu.roll(value, (span - far) % span, 1) * table[row + 1 : row + 2, :]
        if bricks[axis] > 1:
            result = result + pltpu.roll(value, (span - near) % span, 1) * table[row : row + 1, :]
        return result

    def all_ahead(value):
        result = []
        by_z = {0: value}
        by_yz = {}
        for dx, dy, dz in OFFSETS:
            if dz not in by_z:
                by_z[dz] = pull(value, 2, dz)
            if (dy, dz) not in by_yz:
                by_yz[dy, dz] = pull(by_z[dz], 1, dy) if dy else by_z[dz]
            result.append(pull(by_yz[dy, dz], 0, dx) if dx else by_yz[dy, dz])
        return result

    def fold(read):
        by_yz = {}
        for d, (dx, dy, dz) in enumerate(OFFSETS):
            term = read(d)
            term = pull(term, 0, -dx) if dx else term
            by_yz[dy, dz] = by_yz[dy, dz] + term if (dy, dz) in by_yz else term
        by_z = {}
        for (dy, dz), term in by_yz.items():
            term = pull(term, 1, -dy) if dy else term
            by_z[dz] = by_z[dz] + term if dz in by_z else term
        total = None
        for dz, term in by_z.items():
            term = pull(term, 2, -dz) if dz else term
            total = term if total is None else total + term
        return total

    def operate(vector, shifted):
        for d, value in enumerate(all_ahead(vector)):
            ahead[d] = value
        ahead[DIRS] = vector

        def forward(a, carry):
            total = blocks[0, a] * ahead[0]
            for d in range(1, DIRS + 1):
                total = total + blocks[d, a] * ahead[d]
            image[pl.ds(a, 1), :] = jnp.sum(total, axis=0, keepdims=True)
            return carry

        lax.fori_loop(0, 12, forward, 0)
        if shifted is None:

            def backward(d, carry):
                total = blocks[d, 0] * vector[0:1]
                for a in range(1, 12):
                    total = total + blocks[d, a] * vector[a : a + 1]
                sent[d] = total
                return carry

            lax.fori_loop(0, DIRS, backward, 0)
        else:
            for d in range(DIRS):
                total = None
                for a in range(12):
                    scale = vector[a : a + 1]
                    if a % 4 == 3 and OFFSETS[d][a // 4]:
                        scale = scale - SPACING * OFFSETS[d][a // 4]
                    term = blocks[d, a] * scale
                    total = term if total is None else total + term
                sent[d] = total
        return image[...] + fold(lambda d: sent[d])

    image[...] = jnp.zeros_like(image)
    no_rows = jnp.zeros((4, span), jnp.float32)

    def expand(d, carry):
        for c in range(3):
            for e in range(4):
                for k in range(3):
                    first = normal_pair(c, k) * 16 + e * 4
                    blocks[d, 4 * c + e, 4 * k : 4 * k + 4, :] = -parts[d, first : first + 4, :]
                blocks[d, 4 * c + e, 12:16, :] = no_rows
        return carry

    lax.fori_loop(0, DIRS, expand, 0)
    diag = parts[DIRS, PAIR_ROWS:ROWS, :] + fold(lambda d: parts[d, PAIR_ROWS:ROWS, :])
    for c in range(3):
        for e in range(4):
            for k in range(3):
                for f in range(4):
                    row = normal_pair(c, k) * 10 + point_pair(e, f)
                    blocks[DIRS, 4 * c + e, 4 * k + f : 4 * k + f + 1, :] = diag[row : row + 1]
            blocks[DIRS, 4 * c + e, 12:16, :] = no_rows

    rank = lax.broadcasted_iota(jnp.int32, (16, span), 0)
    unit = ((rank == 0) | (rank == 5) | (rank == 10)).astype(jnp.float32)
    keep = (table[12:13, :] != anchor[0].astype(jnp.float32)).astype(jnp.float32)
    matrix = parts[DIRS + 1, 0:16, :] + unit
    grad = operate(matrix, True) - SPACING * parts[DIRS + 2, 0:16, :]
    rhs = -(keep * grad)

    keep_all = jnp.broadcast_to(keep, (8, span))
    for d, value in enumerate(all_ahead(keep_all)):
        both = keep * value[0:1]

        def mask(a, carry, d=d, both=both):
            blocks[d, a] = blocks[d, a] * both
            return carry

        lax.fori_loop(0, 12, mask, 0)
    rows = []
    for a in range(12):
        eye = (rank == a).astype(jnp.float32)
        row = keep * (blocks[DIRS, a] + DAMPING * eye) + (1.0 - keep) * eye
        blocks[DIRS, a] = row
        inverse[a] = row
    for pivot in range(12):
        here = inverse[pivot]
        factor = 1.0 / here[pivot : pivot + 1]
        at_pivot = rank == pivot
        scaled_row = jnp.where(at_pivot, factor, here * factor)
        for a in range(12):
            if a == pivot:
                inverse[a] = scaled_row
            else:
                row = inverse[a]
                column = row[pivot : pivot + 1]
                inverse[a] = jnp.where(at_pivot, 0.0, row) - column * scaled_row

    def precondition(vector):
        parts_of = [jnp.sum(inverse[a] * vector, axis=0, keepdims=True) for a in range(12)]
        return jnp.concatenate(parts_of + [no_rows], axis=0)

    def dot(left, right):
        return jnp.sum(left * right, keepdims=True)

    first = precondition(rhs)

    def step(_, carry):
        update, residual, direction, inner_now = carry
        along = operate(direction, None)
        alpha = inner_now / dot(direction, along)
        update = update + alpha * direction
        residual = residual - alpha * along
        scaled = precondition(residual)
        inner_next = dot(residual, scaled)
        direction = scaled + (inner_next / inner_now) * direction
        return update, residual, direction, inner_next

    start = (jnp.zeros_like(rhs), rhs, first, dot(rhs, first))
    update, residual, _, _ = lax.fori_loop(0, ITERS, step, start)
    update_out[...] = update
    residual_out[...] = residual


def lane_masks(bricks, devices):
    shape = tuple(devices) + tuple(bricks)
    index = np.indices(shape).reshape(6, -1)
    table = np.zeros((16, index.shape[1]), np.float32)
    flat = 0
    for axis in range(3):
        outer, inner = index[axis], index[3 + axis]
        end = inner == bricks[axis] - 1
        table[4 * axis] = ~end
        table[4 * axis + 1] = end & (outer < devices[axis] - 1)
        table[4 * axis + 2] = inner > 0
        table[4 * axis + 3] = (inner == 0) & (outer > 0)
        flat = flat * (devices[axis] * bricks[axis]) + outer * bricks[axis] + inner
    table[12] = flat
    return table


def on_device(source_points, target_points, normals, weights, blocks, affines, anchor):
    bricks = source_points.shape[2:5]
    points = source_points.shape[5]
    devices = tuple(lax.axis_size(name) for name in AXES)
    count = devices[0] * devices[1] * devices[2]
    tiles = bricks[0] * bricks[1] * bricks[2]
    width = SLOTS * tiles
    span = count * tiles
    params = functools.partial(pltpu.CompilerParams, vmem_limit_bytes=VMEM_BYTES)
    vmem = pl.BlockSpec(memory_space=pltpu.VMEM)

    inside = jnp.ones((DIRS,) + bricks, jnp.float32)
    for axis, name in enumerate(AXES):
        spots = lax.axis_index(name) * bricks[axis] + np.arange(bricks[axis], dtype=np.int32)
        total = devices[axis] * bricks[axis]
        steps = np.array([offset[axis] for offset in OFFSETS], np.int32).reshape(-1, 1)
        ahead = spots.reshape(1, -1) + steps
        fits = ((ahead >= 0) & (ahead < total)).astype(jnp.float32)
        inside = inside * fits.reshape((DIRS,) + tuple(-1 if i == axis else 1 for i in range(3)))
    limit = (BLOCK * blocks.astype(jnp.float32) * inside).reshape(1, DIRS * tiles)
    strides = np.repeat(np.array(OFFSETS, np.float32).T, tiles, axis=1)
    lane_table = jnp.concatenate(
        [jnp.asarray(strides), limit, jnp.zeros((4, DIRS * tiles), jnp.float32)]
    )
    lane_table = jnp.pad(lane_table, ((0, 0), (0, width - DIRS * tiles)))
    affine = jnp.pad(
        affines.reshape(12, tiles), ((0, 4), ((DIRS + 1) * tiles, width - (DIRS + 2) * tiles))
    )

    def flat(value):
        lead = value.shape[:-5]
        value = value.reshape(lead + (DIRS * tiles, points))
        return jnp.pad(value, ((0, 0),) * len(lead) + ((0, width - DIRS * tiles), (0, 0)))

    local = pl.pallas_call(
        functools.partial(assemble_kernel, tiles),
        out_shape=jax.ShapeDtypeStruct((ROWS, width), jnp.float32),
        in_specs=[vmem] * 6,
        out_specs=vmem,
        scratch_shapes=[
            pltpu.VMEM((10, points, width), jnp.float32),
            pltpu.VMEM((ROWS + BACK_ROWS, 8, width), jnp.float32),
        ],
        compiler_params=params(),
        name="assemble",
    )(
        flat(source_points),
        flat(moved_targets(target_points)),
        flat(normals),
        flat(weights),
        lane_table,
        affine,
    )
    chips = count // 2
    gathered = pl.pallas_call(
        functools.partial(gather_kernel, devices),
        out_shape=jax.ShapeDtypeStruct((count, ROWS, width), jnp.float32),
        in_specs=[vmem],
        out_specs=vmem,
        scratch_shapes=[pltpu.SemaphoreType.DMA] + [pltpu.SemaphoreType.DMA((chips,))] * 4,
        compiler_params=params(collective_id=0, has_side_effects=True),
        name="gather",
    )(local)
    parts = pl.pallas_call(
        functools.partial(turn_kernel, tiles),
        grid=(count // SLOTS,),
        out_shape=jax.ShapeDtypeStruct((SLOTS, ROWS, span), jnp.float32),
        in_specs=[pl.BlockSpec((SLOTS, ROWS, width), lambda g: (g, 0, 0))],
        out_specs=pl.BlockSpec((SLOTS, ROWS, width), lambda g: (0, 0, g)),
        compiler_params=params(),
        name="turn",
    )(gathered)
    update, residual = pl.pallas_call(
        functools.partial(solve_kernel, bricks, devices),
        out_shape=[jax.ShapeDtypeStruct((16, span), jnp.float32)] * 2,
        in_specs=[pl.BlockSpec(memory_space=pltpu.SMEM), vmem, vmem],
        out_specs=[vmem, vmem],
        scratch_shapes=[
            pltpu.VMEM((DIRS + 1, 12, 16, span), jnp.float32),
            pltpu.VMEM((12, 16, span), jnp.float32),
            pltpu.VMEM((DIRS + 1, 16, span), jnp.float32),
            pltpu.VMEM((DIRS, 16, span), jnp.float32),
            pltpu.VMEM((16, span), jnp.float32),
        ],
        compiler_params=params(),
        name="solve",
    )(anchor, parts, jnp.asarray(lane_masks(bricks, devices)))
    me = (lax.axis_index("gx") * devices[1] + lax.axis_index("gy")) * devices[2]
    me = me + lax.axis_index("gz")

    def mine(value):
        return lax.dynamic_slice(value, (0, me * tiles), (12, tiles)).reshape((12,) + bricks)

    return mine(update), mine(residual)


def solution(mesh):
    placed = (
        P(None, None, "gx", "gy", "gz", None),
        P(None, None, "gx", "gy", "gz", None),
        P(None, None, "gx", "gy", "gz", None),
        P(None, "gx", "gy", "gz", None),
        P(None, "gx", "gy", "gz"),
        P(None, "gx", "gy", "gz"),
        P(),
    )
    return jax.shard_map(
        on_device,
        mesh=mesh,
        in_specs=placed,
        out_specs=(P(None, "gx", "gy", "gz"), P(None, "gx", "gy", "gz")),
        check_vma=False,
    )
```

time: 1320 us -> 120 us (0.09); the launches traced: 1300 us -> 120 us
  blocking collectives: 405 us -> 0 us
  starting transfers between devices: 382 us -> 16.3 us
  matrix products: 170 us -> 0 us
  local copies, waits for them, and re-layouts: 174 us -> 12.3 us
  Pallas kernels: 0 us -> 83.1 us
  other arithmetic: 75 us -> 3.79 us
  waiting for transfers between devices: 47.6 us -> 2.32 us
  between operations: 46.2 us -> 1.94 us
    psum x10 -> x0, blocking collectives: 405 us -> none  [both_products(): lax.psum((jnp.sum(residual * scaled), jnp.sum(image * scaled)), ('gx', 'g...]
    ppermute x138 -> x6, starting transfers between devices: 382 us -> 16.3 us  [moved_targets(): came = lax.ppermute(slab, name, links)]
    dot_general x131 -> x0, matrix products: 170 us -> none  [the longest x10 56.8 us: operate(): sent = jnp.einsum('dbaxyz,bxyz->daxyz', coupling, vector, precision=exact)]
    pallas_call x0 -> x4, Pallas kernels: none -> 83.1 us  [the longest x1 41.2 us: on_device(): pl.pallas_call(functools.partial(gather_kernel, devices), out_shape=jax.S...]
    mul x72 -> x1, local copies, waits for them, and re-layouts: 52 us -> 0.12 us  [on_device(): BLOCK * blocks.astype(jnp.float32) * inside]
    ppermute x138 -> x6, waiting for transfers between devices: 47.6 us -> 2.32 us  [moved_targets(): came = lax.ppermute(slab, name, links)]
    scatter-add x76 -> x0, local copies, waits for them, and re-layouts: 28.5 us -> none  [the longest x50 23.3 us: operate(): back = back.at[spot(offset, 4, 1, lengths)].add(sent[index])]
    another operation x75 -> x6, local copies, waits for them, and re-layouts: 28.2 us -> 0.43 us  [the longest x1 0.38 us: moved_targets(): return jnp.stack([views[d] for d in range(DIRS)], axis=1)]
  transfers between devices with their start and end apart: 138 -> 6, of which waited for: 32 -> 2; matrix products, arithmetic and copies ran while one was open for 22% -> 7% of each run, Pallas kernels for 0% -> 0%
where the time goes in v1:
time: 120 us
  Pallas kernels  83.1 us (69%)
  starting transfers between devices  16.3 us (14%)
  local copies, waits for them, and re-layouts  12.3 us (10%)
  other arithmetic  3.79 us (3%)
  waiting for transfers between devices  2.32 us (2%)
  between operations  1.94 us (2%)
    pallas_call x1, Pallas kernels, on_device(): pl.pallas_call(functools.partial(gather_kernel, devices), out_shape=jax.S...  41.2 us
    pallas_call x1, Pallas kernels, on_device(): pl.pallas_call(functools.partial(solve_kernel, bricks, devices), out_shap...  20.6 us
    ppermute x6, starting transfers between devices, moved_targets(): came = lax.ppermute(slab, name, links)  16.3 us
    pallas_call x1, Pallas kernels, on_device(): pl.pallas_call(functools.partial(turn_kernel, tiles), grid=(count // SLOT...  14.6 us
    pallas_call x1, Pallas kernels, on_device(): pl.pallas_call(functools.partial(assemble_kernel, tiles), out_shape=jax.S...  6.83 us
    pad x4, local copies, waits for them, and re-layouts, flat(): jnp.pad(value, ((0, 0),) * len(lead) + ((0, width - DIRS * tiles), (0, 0)))  3.75 us
    dynamic_slice x4, local copies, waits for them, and re-layouts, mine(): lax.dynamic_slice(value, (0, me * tiles), (12, tiles))  2.88 us
  transfers between devices with their start and end apart: 6, of which 2 were waited for; matrix products, arithmetic and copies ran while one was open for 7% of the time, Pallas kernels for 0%

profile of v1, /device:TPU:15, one launch (start us, length us, event | category | flops | bytes accessed | tf_op | source)
XLA Modules:
  0.0 119.8 jit_solution(10166728720230894259)
XLA Ops:
  0.7 1.4 %fusion.21 = (f32[3,1,1,4,2,512]{5,4,3,2,1,0:T(2,128)S(1)}, f32[3,1,1,4,2,512]{5,4,3,2,1,0:T(2,128)S(1)}, f32[3,1,1,4,2,512]{5,4,3,2,1,0:T(2,128)S(1)}, f32[3,1,...) fusion(f32[3,13,1,4,2,512]{5,4,3,2,1,0:T(2,128)} %param.16), kind=kLoop, calls=%fused_computation.143 | loop fusion | bytes 1277952 | tf_op jit(solution)/shard_map/slice | solution.py:52
  2.2 3.3 %collective-permute-start.1 = (f32[2,3,1,4,2,512]{5,4,1,3,2,0:T(2,128)S(1)}, f32[2,3,1,4,2,512]{5,4,1,3,2,0:T(2,128)S(1)}, u32[]{:S(2)}, u32[]{:S(2)}) collective-permute-start(f32[2,3,1,4,2,512]{5,4,1,3,2,0:T(2,128)S(1)} %pad_maximum_fusion), channel_id=1, source_target_pairs={{0,8},{8,16},{16,24},{1,9},{9,17},{17,25},{2,10},{10,18},{18,26},{... | collective-permute-start | bytes 294920 | tf_op jit(solution)/shard_map/ppermute | solution.py:69
  5.6 2.1 %collective-permute-start = (f32[7,3,1,4,2,512]{5,4,1,3,2,0:T(2,128)S(1)}, f32[7,3,1,4,2,512]{5,4,1,3,2,0:T(2,128)S(1)}, u32[]{:S(2)}, u32[]{:S(2)}) collective-permute-start(f32[7,3,1,4,2,512]{5,4,1,3,2,0:T(2,128)S(1)} %constant_dynamic-update-slice_fusion), channel_id=1, source_target_pairs={{8,0},{16,8},{24,16},{9,1},{17,9},{25,17},{10,2},{18,10},{26,18},{... | collective-permute-start | bytes 1032200 | tf_op jit(solution)/shard_map/ppermute | solution.py:69
  7.7 0.7 fusion.20
  8.4 0.7 and_convert_fusion
  9.1 0.7 fusion.19
  9.9 0.7 multiply_multiply_fusion
  11.8 0.7 pad.27.affine
  12.5 0.6 pad.26.lane_table
  13.1 0.1 reshape.115
  13.2 0.7 pad.25.weight
  14.0 0.4 reshape.112
  14.4 1.0 pad.22.source
  15.4 0.4 reshape.114
  15.8 1.0 pad.24.normal
  17.1 1.3 %collective-permute-start.3 = (f32[2,3,1,1,2,512]{5,4,1,3,2,0:T(2,128)S(1)}, f32[2,3,1,1,2,512]{5,4,1,3,2,0:T(2,128)S(1)}, u32[]{:S(2)}, u32[]{:S(2)}) collective-permute-start(f32[2,3,1,1,2,512]{5,4,1,3,2,0:T(2,128)S(1)} %pad_maximum_fusion.8), channel_id=1, source_target_pairs={{0,2},{2,4},{4,6},{1,3},{3,5},{5,7},{8,10},{10,12},{12,14},{9,11},... | collective-permute-start | bytes 73736 | tf_op jit(solution)/shard_map/ppermute | solution.py:69
  18.5 4.0 %collective-permute-start.2 = (f32[7,3,1,1,2,512]{5,4,1,3,2,0:T(2,128)S(1)}, f32[7,3,1,1,2,512]{5,4,1,3,2,0:T(2,128)S(1)}, u32[]{:S(2)}, u32[]{:S(2)}) collective-permute-start(f32[7,3,1,1,2,512]{5,4,1,3,2,0:T(2,128)S(1)} %constant_dynamic-update-slice_fusion.7), channel_id=1, source_target_pairs={{2,0},{4,2},{6,4},{3,1},{5,3},{7,5},{10,8},{12,10},{14,12},{11,9},... | collective-permute-start | bytes 258056 | tf_op jit(solution)/shard_map/ppermute | solution.py:69
  22.6 1.4 %collective-permute-done.2 = f32[7,3,1,1,2,512]{5,4,1,3,2,0:T(2,128)S(1)} collective-permute-done((f32[7,3,1,1,2,512]{5,4,1,3,2,0:T(2,128)S(1)}, f32[7,3,1,1,2,512]{5,4,1,3,2,0:T(2,128)S(1)}, u32[]{:S(2)}, u32[]{:S(2)}) %collective-permute-start.2) | collective-permute-done | bytes 86048 | tf_op jit(solution)/shard_map/ppermute | solution.py:69
  24.2 1.3 %collective-permute-start.5 = (f32[2,3,1,4,1,512]{5,3,1,4,2,0:T(4,128)S(1)}, f32[2,3,1,4,1,512]{5,3,1,4,2,0:T(4,128)S(1)}, u32[]{:S(2)}, u32[]{:S(2)}) collective-permute-start(f32[2,3,1,4,1,512]{5,3,1,4,2,0:T(4,128)S(1)} %pad_maximum_fusion.7), channel_id=1, source_target_pairs={{0,1},{2,3},{4,5},{6,7},{8,9},{10,11},{12,13},{14,15},{16,17},{18,... | collective-permute-start | bytes 147464 | tf_op jit(solution)/shard_map/ppermute | solution.py:69
  25.7 4.3 %collective-permute-start.4 = (f32[7,3,1,4,1,512]{5,3,1,4,2,0:T(4,128)S(1)}, f32[7,3,1,4,1,512]{5,3,1,4,2,0:T(4,128)S(1)}, u32[]{:S(2)}, u32[]{:S(2)}) collective-permute-start(f32[7,3,1,4,1,512]{5,3,1,4,2,0:T(4,128)S(1)} %constant_dynamic-update-slice_fusion.14), channel_id=1, source_target_pairs={{1,0},{3,2},{5,4},{7,6},{9,8},{11,10},{13,12},{15,14},{17,16},{19,... | collective-permute-start | bytes 516104 | tf_op jit(solution)/shard_map/ppermute | solution.py:69
  30.1 0.9 collective-permute-done.4
  31.9 0.4 copy.815
  32.3 0.4 reshape.113
  32.7 1.0 pad.23.target
  33.8 6.8 %assemble.1.mine = f32[160,128]{1,0:T(8,128)} custom-call(f32[3,128,512]{2,1,0:T(8,128)} %pad.22.source, f32[3,128,512]{2,1,0:T(8,128)} %pad.23.target, f32[3,128,512]{2,1,0:T(8,128)} %pad.24.normal, f32[128,512]{1,0:T(8,128)} %pad.25.weight, f32[8,128]{1,0:T(8,128)} %pad.26.lane_table, f32[16,128]{1,0:T(8,128)} %pad.27.affine), custom_call_target="tpu_custom_call" | custom-call | tf_op jit(solution)/shard_map/assemble/pallas_call | solution.py:485
  40.6 41.2 %gather.1.gathered = f32[32,160,128]{2,1,0:T(8,128)} custom-call(f32[160,128]{1,0:T(8,128)} %assemble.1.mine), custom_call_target="tpu_custom_call" | custom-call | tf_op jit(solution)/shard_map/gather/pallas_call | solution.py:505
  81.8 14.6 %turn.1.parts = f32[16,160,256]{2,1,0:T(8,128)} custom-call(f32[32,160,128]{2,1,0:T(8,128)} %gather.1.gathered), custom_call_target="tpu_custom_call" | custom-call | tf_op jit(solution)/shard_map/turn/pallas_call | solution.py:514
  96.4 20.6 %solve.1 = (f32[16,256]{1,0:T(8,128)}, f32[16,256]{1,0:T(8,128)}) custom-call(s32[1]{0:T(128)S(6)} %copy.903.anchor, f32[16,160,256]{2,1,0:T(8,128)} %turn.1.parts, f32[16,256]{1,0:T(8,128)} %constant.54.clone.table), custom_call_target="tpu_custom_call" | custom-call | tf_op jit(solution)/shard_map/solve/pallas_call | solution.py:523
  116.9 0.8 constant_dynamic-slice_fusion.1
  117.7 0.8 constant_dynamic-slice_fusion
  118.5 0.7 copy.819
  119.1 0.7 copy.818
  (99 shorter events, 2.2 us)
Async XLA Ops:
  0.6 10.4 %copy-start.4 = (f32[3,104]{1,0:T(4,128)S(1)}, f32[3,104]{1,0:T(4,128)}, u32[]{:S(2)}) copy-start(f32[3,104]{1,0:T(4,128)} %constant.53.clone) | copy-start | bytes 3748
  0.6 11.1 %copy-start.3 = (f32[12,1,4,2]{0,3,2,1:T(2,128)S(1)}, f32[12,1,4,2]{0,3,2,1:T(2,128)}, u32[]{:S(2)}) copy-start(f32[12,1,4,2]{0,3,2,1:T(2,128)} %param.20) | copy-start | bytes 1156
  0.7 12.4 %copy-start.2 = (f32[13,1,4,2,512]{4,3,2,1,0:T(2,128)S(1)}, f32[13,1,4,2,512]{4,3,2,1,0:T(2,128)}, u32[]{:S(2)}) copy-start(f32[13,1,4,2,512]{4,3,2,1,0:T(2,128)} %param.18) | copy-start | bytes 638980
  0.7 13.3 %copy-start = (f32[3,13,1,4,2,512]{5,4,3,2,1,0:T(2,128)S(1)}, f32[3,13,1,4,2,512]{5,4,3,2,1,0:T(2,128)}, u32[]{:S(2)}) copy-start(f32[3,13,1,4,2,512]{5,4,3,2,1,0:T(2,128)} %param.15) | copy-start | bytes 1916932
  2.1 13.3 %copy-start.1 = (f32[3,13,1,4,2,512]{5,4,3,2,1,0:T(2,128)S(1)}, f32[3,13,1,4,2,512]{5,4,3,2,1,0:T(2,128)}, u32[]{:S(2)}) copy-start(f32[3,13,1,4,2,512]{5,4,3,2,1,0:T(2,128)} %param.17) | copy-start | bytes 1916932
  2.2 14.7 %collective-permute-start.1 = (f32[2,3,1,4,2,512]{5,4,1,3,2,0:T(2,128)S(1)}, f32[2,3,1,4,2,512]{5,4,1,3,2,0:T(2,128)S(1)}, u32[]{:S(2)}, u32[]{:S(2)}) collective-permute-start(f32[2,3,1,4,2,512]{5,4,1,3,2,0:T(2,128)S(1)} %pad_maximum_fusion), channel_id=1, source_target_pairs={{0,8},{8,16},{16,24},{1,9},{9,17},{17,25},{2,10},{10,18},{18,26},{... | collective-permute-start | bytes 294920 | tf_op jit(solution)/shard_map/ppermute | solution.py:69
  5.6 11.3 %collective-permute-start = (f32[7,3,1,4,2,512]{5,4,1,3,2,0:T(2,128)S(1)}, f32[7,3,1,4,2,512]{5,4,1,3,2,0:T(2,128)S(1)}, u32[]{:S(2)}, u32[]{:S(2)}) collective-permute-start(f32[7,3,1,4,2,512]{5,4,1,3,2,0:T(2,128)S(1)} %constant_dynamic-update-slice_fusion), channel_id=1, source_target_pairs={{8,0},{16,8},{24,16},{9,1},{17,9},{25,17},{10,2},{18,10},{26,18},{... | collective-permute-start | bytes 1032200 | tf_op jit(solution)/shard_map/ppermute | solution.py:69
  17.1 5.4 %collective-permute-start.3 = (f32[2,3,1,1,2,512]{5,4,1,3,2,0:T(2,128)S(1)}, f32[2,3,1,1,2,512]{5,4,1,3,2,0:T(2,128)S(1)}, u32[]{:S(2)}, u32[]{:S(2)}) collective-permute-start(f32[2,3,1,1,2,512]{5,4,1,3,2,0:T(2,128)S(1)} %pad_maximum_fusion.8), channel_id=1, source_target_pairs={{0,2},{2,4},{4,6},{1,3},{3,5},{5,7},{8,10},{10,12},{12,14},{9,11},... | collective-permute-start | bytes 73736 | tf_op jit(solution)/shard_map/ppermute | solution.py:69
  18.5 5.5 %collective-permute-start.2 = (f32[7,3,1,1,2,512]{5,4,1,3,2,0:T(2,128)S(1)}, f32[7,3,1,1,2,512]{5,4,1,3,2,0:T(2,128)S(1)}, u32[]{:S(2)}, u32[]{:S(2)}) collective-permute-start(f32[7,3,1,1,2,512]{5,4,1,3,2,0:T(2,128)S(1)} %constant_dynamic-update-slice_fusion.7), channel_id=1, source_target_pairs={{2,0},{4,2},{6,4},{3,1},{5,3},{7,5},{10,8},{12,10},{14,12},{11,9},... | collective-permute-start | bytes 258056 | tf_op jit(solution)/shard_map/ppermute | solution.py:69
  24.2 5.8 %collective-permute-start.5 = (f32[2,3,1,4,1,512]{5,3,1,4,2,0:T(4,128)S(1)}, f32[2,3,1,4,1,512]{5,3,1,4,2,0:T(4,128)S(1)}, u32[]{:S(2)}, u32[]{:S(2)}) collective-permute-start(f32[2,3,1,4,1,512]{5,3,1,4,2,0:T(4,128)S(1)} %pad_maximum_fusion.7), channel_id=1, source_target_pairs={{0,1},{2,3},{4,5},{6,7},{8,9},{10,11},{12,13},{14,15},{16,17},{18,... | collective-permute-start | bytes 147464 | tf_op jit(solution)/shard_map/ppermute | solution.py:69
  25.7 5.3 %collective-permute-start.4 = (f32[7,3,1,4,1,512]{5,3,1,4,2,0:T(4,128)S(1)}, f32[7,3,1,4,1,512]{5,3,1,4,2,0:T(4,128)S(1)}, u32[]{:S(2)}, u32[]{:S(2)}) collective-permute-start(f32[7,3,1,4,1,512]{5,3,1,4,2,0:T(4,128)S(1)} %constant_dynamic-update-slice_fusion.14), channel_id=1, source_target_pairs={{1,0},{3,2},{5,4},{7,6},{9,8},{11,10},{13,12},{15,14},{17,16},{19,... | collective-permute-start | bytes 516104 | tf_op jit(solution)/shard_map/ppermute | solution.py:69

commit v2 on v1

--- a/solution.py
+++ b/solution.py
@@ -46,6 +46,18 @@
 
 def point_pair(e, k):
     return POINT_PAIRS.index((min(e, k), max(e, k)))
+
+
+def grouped(count, group, body):
+    def trip(i, carry):
+        for j in range(group):
+            body(i * group + j)
+        return carry
+
+    whole = count // group
+    lax.fori_loop(0, whole, trip, 0)
+    for i in range(whole * group, count):
+        body(i)
 
 
 def moved_targets(target):
@@ -245,7 +257,7 @@
 def turn_kernel(tiles, gathered, out):
     width = gathered.shape[2]
 
-    def body(chunk, carry):
+    def body(chunk):
         rows = pl.ds(pl.multiple_of(chunk * 8, 8), 8)
         slot = lax.broadcasted_iota(jnp.int32, (8, width), 1) // tiles
         values = [gathered[j, rows, :] for j in range(SLOTS)]
@@ -263,9 +275,8 @@
             values = fresh
         for j in range(SLOTS):
             out[j, rows, :] = values[j]
-        return carry
-
-    lax.fori_loop(0, ROWS // 8, body, 0)
+
+    grouped(ROWS // 8, 5, body)
 
 
 def solve_kernel(
@@ -273,6 +284,7 @@
 ):
     span = parts.shape[2]
     tiles = bricks[0] * bricks[1] * bricks[2]
+    group = 4 if span <= 512 else 1
     inner = (bricks[1] * bricks[2], bricks[2], 1)
     outer = (devices[1] * devices[2] * tiles, devices[2] * tiles, tiles)
 
@@ -318,24 +330,22 @@
             ahead[d] = value
         ahead[DIRS] = vector
 
-        def forward(a, carry):
+        def forward(a):
             total = blocks[0, a] * ahead[0]
             for d in range(1, DIRS + 1):
                 total = total + blocks[d, a] * ahead[d]
             image[pl.ds(a, 1), :] = jnp.sum(total, axis=0, keepdims=True)
-            return carry
-
-        lax.fori_loop(0, 12, forward, 0)
+
+        grouped(12, group, forward)
         if shifted is None:
 
-            def backward(d, carry):
+            def backward(d):
                 total = blocks[d, 0] * vector[0:1]
                 for a in range(1, 12):
                     total = total + blocks[d, a] * vector[a : a + 1]
                 sent[d] = total
-                return carry
-
-            lax.fori_loop(0, DIRS, backward, 0)
+
+            grouped(DIRS, group, backward)
         else:
             for d in range(DIRS):
                 total = None
@@ -506,7 +516,7 @@
         functools.partial(gather_kernel, devices),
         out_shape=jax.ShapeDtypeStruct((count, ROWS, width), jnp.float32),
         in_specs=[vmem],
-        out_specs=vmem,
+        out_specs=pl.BlockSpec(memory_space=pl.ANY),
         scratch_shapes=[pltpu.SemaphoreType.DMA] + [pltpu.SemaphoreType.DMA((chips,))] * 4,
         compiler_params=params(collective_id=0, has_side_effects=True),
         name="gather",

time: 120 us -> 109 us (0.908)
  Pallas kernels: 83.1 us -> 72 us
    pallas_call x1, Pallas kernels: 14.6 us -> 7.56 us  [on_device(): pl.pallas_call(functools.partial(turn_kernel, tiles), grid=(count // SLOT...]
    pallas_call x1, Pallas kernels: 20.6 us -> 17.7 us  [on_device(): pl.pallas_call(functools.partial(solve_kernel, bricks, devices), out_shap...]
    pallas_call x1, Pallas kernels: 41.2 us -> 39.9 us  [on_device(): pl.pallas_call(functools.partial(gather_kernel, devices), out_shape=jax.S...]
  transfers between devices with their start and end apart: 6 -> 6, of which waited for: 2 -> 2; matrix products, arithmetic and copies ran while one was open for 7% -> 8% of each run, Pallas kernels for 0% -> 0%
where the time goes in v2:
time: 109 us
  Pallas kernels  72 us (66%)
  starting transfers between devices  16.3 us (15%)
  local copies, waits for them, and re-layouts  12.3 us (11%)
  other arithmetic  3.79 us (3%)
  waiting for transfers between devices  2.32 us (2%)
  between operations  1.94 us (2%)
    pallas_call x1, Pallas kernels, on_device(): pl.pallas_call(functools.partial(gather_kernel, devices), out_shape=jax.S...  39.9 us
    pallas_call x1, Pallas kernels, on_device(): pl.pallas_call(functools.partial(solve_kernel, bricks, devices), out_shap...  17.7 us
    ppermute x6, starting transfers between devices, moved_targets(): came = lax.ppermute(slab, name, links)  16.3 us
    pallas_call x1, Pallas kernels, on_device(): pl.pallas_call(functools.partial(turn_kernel, tiles), grid=(count // SLOT...  7.56 us
    pallas_call x1, Pallas kernels, on_device(): pl.pallas_call(functools.partial(assemble_kernel, tiles), out_shape=jax.S...  6.83 us
    pad x4, local copies, waits for them, and re-layouts, flat(): jnp.pad(value, ((0, 0),) * len(lead) + ((0, width - DIRS * tiles), (0, 0)))  3.75 us
    dynamic_slice x4, local copies, waits for them, and re-layouts, mine(): lax.dynamic_slice(value, (0, me * tiles), (12, tiles))  2.88 us
    ppermute x6, waiting for transfers between devices, moved_targets(): came = lax.ppermute(slab, name, links)  2.32 us
  transfers between devices with their start and end apart: 6, of which 2 were waited for; matrix products, arithmetic and copies ran while one was open for 8% of the time, Pallas kernels for 0%

profile of v2, /device:TPU:15, one launch (start us, length us, event | category | flops | bytes accessed | tf_op | source)
XLA Modules:
  0.0 108.7 jit_solution(10993913912224131339)
XLA Ops:
  0.7 1.4 %fusion.21 = (f32[3,1,1,4,2,512]{5,4,3,2,1,0:T(2,128)S(1)}, f32[3,1,1,4,2,512]{5,4,3,2,1,0:T(2,128)S(1)}, f32[3,1,1,4,2,512]{5,4,3,2,1,0:T(2,128)S(1)}, f32[3,1,...) fusion(f32[3,13,1,4,2,512]{5,4,3,2,1,0:T(2,128)} %param.16), kind=kLoop, calls=%fused_computation.143 | loop fusion | bytes 1277952 | tf_op jit(solution)/shard_map/slice | solution.py:64
  2.2 3.3 %collective-permute-start.1 = (f32[2,3,1,4,2,512]{5,4,1,3,2,0:T(2,128)S(1)}, f32[2,3,1,4,2,512]{5,4,1,3,2,0:T(2,128)S(1)}, u32[]{:S(2)}, u32[]{:S(2)}) collective-permute-start(f32[2,3,1,4,2,512]{5,4,1,3,2,0:T(2,128)S(1)} %pad_maximum_fusion), channel_id=1, source_target_pairs={{0,8},{8,16},{16,24},{1,9},{9,17},{17,25},{2,10},{10,18},{18,26},{... | collective-permute-start | bytes 294920 | tf_op jit(solution)/shard_map/ppermute | solution.py:81
  5.6 2.1 %collective-permute-start = (f32[7,3,1,4,2,512]{5,4,1,3,2,0:T(2,128)S(1)}, f32[7,3,1,4,2,512]{5,4,1,3,2,0:T(2,128)S(1)}, u32[]{:S(2)}, u32[]{:S(2)}) collective-permute-start(f32[7,3,1,4,2,512]{5,4,1,3,2,0:T(2,128)S(1)} %constant_dynamic-update-slice_fusion), channel_id=1, source_target_pairs={{8,0},{16,8},{24,16},{9,1},{17,9},{25,17},{10,2},{18,10},{26,18},{... | collective-permute-start | bytes 1032200 | tf_op jit(solution)/shard_map/ppermute | solution.py:81
  7.7 0.7 fusion.20
  8.4 0.7 and_convert_fusion
  9.1 0.7 fusion.19
  9.9 0.7 multiply_multiply_fusion
  11.8 0.7 pad.27.affine
  12.5 0.6 pad.26.lane_table
  13.1 0.1 reshape.115
  13.2 0.7 pad.25.weight
  14.0 0.4 reshape.112
  14.4 1.0 pad.22.source
  15.4 0.4 reshape.114
  15.8 1.0 pad.24.normal
  17.1 1.3 %collective-permute-start.3 = (f32[2,3,1,1,2,512]{5,4,1,3,2,0:T(2,128)S(1)}, f32[2,3,1,1,2,512]{5,4,1,3,2,0:T(2,128)S(1)}, u32[]{:S(2)}, u32[]{:S(2)}) collective-permute-start(f32[2,3,1,1,2,512]{5,4,1,3,2,0:T(2,128)S(1)} %pad_maximum_fusion.8), channel_id=1, source_target_pairs={{0,2},{2,4},{4,6},{1,3},{3,5},{5,7},{8,10},{10,12},{12,14},{9,11},... | collective-permute-start | bytes 73736 | tf_op jit(solution)/shard_map/ppermute | solution.py:81
  18.5 4.0 %collective-permute-start.2 = (f32[7,3,1,1,2,512]{5,4,1,3,2,0:T(2,128)S(1)}, f32[7,3,1,1,2,512]{5,4,1,3,2,0:T(2,128)S(1)}, u32[]{:S(2)}, u32[]{:S(2)}) collective-permute-start(f32[7,3,1,1,2,512]{5,4,1,3,2,0:T(2,128)S(1)} %constant_dynamic-update-slice_fusion.7), channel_id=1, source_target_pairs={{2,0},{4,2},{6,4},{3,1},{5,3},{7,5},{10,8},{12,10},{14,12},{11,9},... | collective-permute-start | bytes 258056 | tf_op jit(solution)/shard_map/ppermute | solution.py:81
  22.6 1.4 %collective-permute-done.2 = f32[7,3,1,1,2,512]{5,4,1,3,2,0:T(2,128)S(1)} collective-permute-done((f32[7,3,1,1,2,512]{5,4,1,3,2,0:T(2,128)S(1)}, f32[7,3,1,1,2,512]{5,4,1,3,2,0:T(2,128)S(1)}, u32[]{:S(2)}, u32[]{:S(2)}) %collective-permute-start.2) | collective-permute-done | bytes 86048 | tf_op jit(solution)/shard_map/ppermute | solution.py:81
  24.2 1.3 %collective-permute-start.5 = (f32[2,3,1,4,1,512]{5,3,1,4,2,0:T(4,128)S(1)}, f32[2,3,1,4,1,512]{5,3,1,4,2,0:T(4,128)S(1)}, u32[]{:S(2)}, u32[]{:S(2)}) collective-permute-start(f32[2,3,1,4,1,512]{5,3,1,4,2,0:T(4,128)S(1)} %pad_maximum_fusion.7), channel_id=1, source_target_pairs={{0,1},{2,3},{4,5},{6,7},{8,9},{10,11},{12,13},{14,15},{16,17},{18,... | collective-permute-start | bytes 147464 | tf_op jit(solution)/shard_map/ppermute | solution.py:81
  25.7 4.3 %collective-permute-start.4 = (f32[7,3,1,4,1,512]{5,3,1,4,2,0:T(4,128)S(1)}, f32[7,3,1,4,1,512]{5,3,1,4,2,0:T(4,128)S(1)}, u32[]{:S(2)}, u32[]{:S(2)}) collective-permute-start(f32[7,3,1,4,1,512]{5,3,1,4,2,0:T(4,128)S(1)} %constant_dynamic-update-slice_fusion.14), channel_id=1, source_target_pairs={{1,0},{3,2},{5,4},{7,6},{9,8},{11,10},{13,12},{15,14},{17,16},{19,... | collective-permute-start | bytes 516104 | tf_op jit(solution)/shard_map/ppermute | solution.py:81
  30.1 0.9 collective-permute-done.4
  31.9 0.4 copy.815
  32.3 0.4 reshape.113
  32.7 1.0 pad.23.target
  33.8 6.8 %assemble.1.mine = f32[160,128]{1,0:T(8,128)} custom-call(f32[3,128,512]{2,1,0:T(8,128)} %pad.22.source, f32[3,128,512]{2,1,0:T(8,128)} %pad.23.target, f32[3,128,512]{2,1,0:T(8,128)} %pad.24.normal, f32[128,512]{1,0:T(8,128)} %pad.25.weight, f32[8,128]{1,0:T(8,128)} %pad.26.lane_table, f32[16,128]{1,0:T(8,128)} %pad.27.affine), custom_call_target="tpu_custom_call" | custom-call | tf_op jit(solution)/shard_map/assemble/pallas_call | solution.py:495
  40.6 39.9 %gather.1.gathered = f32[32,160,128]{2,1,0:T(8,128)} custom-call(f32[160,128]{1,0:T(8,128)} %assemble.1.mine), custom_call_target="tpu_custom_call" | custom-call | tf_op jit(solution)/shard_map/gather/pallas_call | solution.py:515
  80.5 7.6 %turn.1.parts = f32[16,160,256]{2,1,0:T(8,128)} custom-call(f32[32,160,128]{2,1,0:T(8,128)} %gather.1.gathered), custom_call_target="tpu_custom_call" | custom-call | tf_op jit(solution)/shard_map/turn/pallas_call | solution.py:524
  88.1 17.7 %solve.1 = (f32[16,256]{1,0:T(8,128)}, f32[16,256]{1,0:T(8,128)}) custom-call(s32[1]{0:T(128)S(6)} %copy.903.anchor, f32[16,160,256]{2,1,0:T(8,128)} %turn.1.parts, f32[16,256]{1,0:T(8,128)} %constant.54.clone.table), custom_call_target="tpu_custom_call" | custom-call | tf_op jit(solution)/shard_map/solve/pallas_call | solution.py:533
  105.8 0.8 constant_dynamic-slice_fusion.1
  106.6 0.8 constant_dynamic-slice_fusion
  107.3 0.7 copy.819
  108.0 0.7 copy.818
  (99 shorter events, 2.2 us)
Async XLA Ops:
  0.6 10.4 %copy-start.4 = (f32[3,104]{1,0:T(4,128)S(1)}, f32[3,104]{1,0:T(4,128)}, u32[]{:S(2)}) copy-start(f32[3,104]{1,0:T(4,128)} %constant.53.clone) | copy-start | bytes 3748
  0.6 11.1 %copy-start.3 = (f32[12,1,4,2]{0,3,2,1:T(2,128)S(1)}, f32[12,1,4,2]{0,3,2,1:T(2,128)}, u32[]{:S(2)}) copy-start(f32[12,1,4,2]{0,3,2,1:T(2,128)} %param.20) | copy-start | bytes 1156
  0.7 12.4 %copy-start.2 = (f32[13,1,4,2,512]{4,3,2,1,0:T(2,128)S(1)}, f32[13,1,4,2,512]{4,3,2,1,0:T(2,128)}, u32[]{:S(2)}) copy-start(f32[13,1,4,2,512]{4,3,2,1,0:T(2,128)} %param.18) | copy-start | bytes 638980
  0.7 13.3 %copy-start = (f32[3,13,1,4,2,512]{5,4,3,2,1,0:T(2,128)S(1)}, f32[3,13,1,4,2,512]{5,4,3,2,1,0:T(2,128)}, u32[]{:S(2)}) copy-start(f32[3,13,1,4,2,512]{5,4,3,2,1,0:T(2,128)} %param.15) | copy-start | bytes 1916932
  2.1 13.3 %copy-start.1 = (f32[3,13,1,4,2,512]{5,4,3,2,1,0:T(2,128)S(1)}, f32[3,13,1,4,2,512]{5,4,3,2,1,0:T(2,128)}, u32[]{:S(2)}) copy-start(f32[3,13,1,4,2,512]{5,4,3,2,1,0:T(2,128)} %param.17) | copy-start | bytes 1916932
  2.2 14.7 %collective-permute-start.1 = (f32[2,3,1,4,2,512]{5,4,1,3,2,0:T(2,128)S(1)}, f32[2,3,1,4,2,512]{5,4,1,3,2,0:T(2,128)S(1)}, u32[]{:S(2)}, u32[]{:S(2)}) collective-permute-start(f32[2,3,1,4,2,512]{5,4,1,3,2,0:T(2,128)S(1)} %pad_maximum_fusion), channel_id=1, source_target_pairs={{0,8},{8,16},{16,24},{1,9},{9,17},{17,25},{2,10},{10,18},{18,26},{... | collective-permute-start | bytes 294920 | tf_op jit(solution)/shard_map/ppermute | solution.py:81
  5.6 11.3 %collective-permute-start = (f32[7,3,1,4,2,512]{5,4,1,3,2,0:T(2,128)S(1)}, f32[7,3,1,4,2,512]{5,4,1,3,2,0:T(2,128)S(1)}, u32[]{:S(2)}, u32[]{:S(2)}) collective-permute-start(f32[7,3,1,4,2,512]{5,4,1,3,2,0:T(2,128)S(1)} %constant_dynamic-update-slice_fusion), channel_id=1, source_target_pairs={{8,0},{16,8},{24,16},{9,1},{17,9},{25,17},{10,2},{18,10},{26,18},{... | collective-permute-start | bytes 1032200 | tf_op jit(solution)/shard_map/ppermute | solution.py:81
  17.1 5.4 %collective-permute-start.3 = (f32[2,3,1,1,2,512]{5,4,1,3,2,0:T(2,128)S(1)}, f32[2,3,1,1,2,512]{5,4,1,3,2,0:T(2,128)S(1)}, u32[]{:S(2)}, u32[]{:S(2)}) collective-permute-start(f32[2,3,1,1,2,512]{5,4,1,3,2,0:T(2,128)S(1)} %pad_maximum_fusion.8), channel_id=1, source_target_pairs={{0,2},{2,4},{4,6},{1,3},{3,5},{5,7},{8,10},{10,12},{12,14},{9,11},... | collective-permute-start | bytes 73736 | tf_op jit(solution)/shard_map/ppermute | solution.py:81
  18.5 5.5 %collective-permute-start.2 = (f32[7,3,1,1,2,512]{5,4,1,3,2,0:T(2,128)S(1)}, f32[7,3,1,1,2,512]{5,4,1,3,2,0:T(2,128)S(1)}, u32[]{:S(2)}, u32[]{:S(2)}) collective-permute-start(f32[7,3,1,1,2,512]{5,4,1,3,2,0:T(2,128)S(1)} %constant_dynamic-update-slice_fusion.7), channel_id=1, source_target_pairs={{2,0},{4,2},{6,4},{3,1},{5,3},{7,5},{10,8},{12,10},{14,12},{11,9},... | collective-permute-start | bytes 258056 | tf_op jit(solution)/shard_map/ppermute | solution.py:81
  24.2 5.8 %collective-permute-start.5 = (f32[2,3,1,4,1,512]{5,3,1,4,2,0:T(4,128)S(1)}, f32[2,3,1,4,1,512]{5,3,1,4,2,0:T(4,128)S(1)}, u32[]{:S(2)}, u32[]{:S(2)}) collective-permute-start(f32[2,3,1,4,1,512]{5,3,1,4,2,0:T(4,128)S(1)} %pad_maximum_fusion.7), channel_id=1, source_target_pairs={{0,1},{2,3},{4,5},{6,7},{8,9},{10,11},{12,13},{14,15},{16,17},{18,... | collective-permute-start | bytes 147464 | tf_op jit(solution)/shard_map/ppermute | solution.py:81
  25.7 5.3 %collective-permute-start.4 = (f32[7,3,1,4,1,512]{5,3,1,4,2,0:T(4,128)S(1)}, f32[7,3,1,4,1,512]{5,3,1,4,2,0:T(4,128)S(1)}, u32[]{:S(2)}, u32[]{:S(2)}) collective-permute-start(f32[7,3,1,4,1,512]{5,3,1,4,2,0:T(4,128)S(1)} %constant_dynamic-update-slice_fusion.14), channel_id=1, source_target_pairs={{1,0},{3,2},{5,4},{7,6},{9,8},{11,10},{13,12},{15,14},{17,16},{19,... | collective-permute-start | bytes 516104 | tf_op jit(solution)/shard_map/ppermute | solution.py:81

commit v3 on v2

--- a/solution.py
+++ b/solution.py
@@ -91,15 +91,20 @@
 
 
 def assemble_kernel(tiles, source, target, normal, weight, lane_table, affine, out, turned, acc):
-    width = source.shape[1]
+    width = SLOTS * tiles
     points = source.shape[2]
+    filling = jnp.zeros((width - DIRS * tiles, 128), jnp.float32)
+
+    def turn(block):
+        return jnp.concatenate([block, filling], axis=0).T
+
     for start in range(0, points, 128):
         spots = pl.ds(start, 128)
         for c in range(3):
-            turned[c, spots, :] = source[c, :, spots].T
-            turned[3 + c, spots, :] = target[c, :, spots].T
-            turned[6 + c, spots, :] = normal[c, :, spots].T
-        turned[9, spots, :] = weight[:, spots].T
+            turned[c, spots, :] = turn(source[c, :, spots])
+            turned[3 + c, spots, :] = turn(target[c, :, spots])
+            turned[6 + c, spots, :] = turn(normal[c, :, spots])
+        turned[9, spots, :] = turn(weight[:, spots])
     acc[...] = jnp.zeros_like(acc)
     step = 32
     limit = lane_table[3:4, :]
@@ -246,8 +251,8 @@
         handed(k).wait()
         return carry
 
+    first_hand().start()
     lax.fori_loop(1, chips, send, 0)
-    first_hand().start()
     lax.fori_loop(1, chips, forward, 0)
     first_hand().wait()
     lax.fori_loop(1, chips, finish, 0)
@@ -284,7 +289,7 @@
 ):
     span = parts.shape[2]
     tiles = bricks[0] * bricks[1] * bricks[2]
-    group = 4 if span <= 512 else 1
+    group = DIRS if span <= 512 else 1
     inner = (bricks[1] * bricks[2], bricks[2], 1)
     outer = (devices[1] * devices[2] * tiles, devices[2] * tiles, tiles)
 
@@ -336,7 +341,7 @@
                 total = total + blocks[d, a] * ahead[d]
             image[pl.ds(a, 1), :] = jnp.sum(total, axis=0, keepdims=True)
 
-        grouped(12, group, forward)
+        grouped(12, min(group, 12), forward)
         if shifted is None:
 
             def backward(d):
@@ -489,8 +494,7 @@
 
     def flat(value):
         lead = value.shape[:-5]
-        value = value.reshape(lead + (DIRS * tiles, points))
-        return jnp.pad(value, ((0, 0),) * len(lead) + ((0, width - DIRS * tiles), (0, 0)))
+        return value.reshape(lead + (DIRS * tiles, points))
 
     local = pl.pallas_call(
         functools.partial(assemble_kernel, tiles),

time: 109 us -> 104 us (0.954)
  Pallas kernels: 72 us -> 67.3 us
    pallas_call x1, Pallas kernels: 17.7 us -> 13.2 us  [on_device(): pl.pallas_call(functools.partial(solve_kernel, bricks, devices), out_shap...]
    pad x4 -> x0, local copies, waits for them, and re-layouts: 3.75 us -> none  [flat(): jnp.pad(value, ((0, 0),) * len(lead) + ((0, width - DIRS * tiles), (0, 0)))]
    reshape x4, local copies, waits for them, and re-layouts: 1.47 us -> 4.69 us  [flat(): return value.reshape(lead + (DIRS * tiles, points))]
where the time goes in v3:
time: 104 us; the launch traced here: 103 us
  Pallas kernels  67.3 us (65%)
  starting transfers between devices  16.3 us (16%)
  local copies, waits for them, and re-layouts  11.8 us (11%)
  other arithmetic  3.79 us (4%)
  waiting for transfers between devices  2.32 us (2%)
  between operations  1.93 us (2%)
    pallas_call x1, Pallas kernels, on_device(): pl.pallas_call(functools.partial(gather_kernel, devices), out_shape=jax.S...  39.8 us
    ppermute x6, starting transfers between devices, moved_targets(): came = lax.ppermute(slab, name, links)  16.3 us
    pallas_call x1, Pallas kernels, on_device(): pl.pallas_call(functools.partial(solve_kernel, bricks, devices), out_shap...  13.2 us
    pallas_call x1, Pallas kernels, on_device(): pl.pallas_call(functools.partial(turn_kernel, tiles), grid=(count // SLOT...  7.56 us
    pallas_call x1, Pallas kernels, on_device(): pl.pallas_call(functools.partial(assemble_kernel, tiles), out_shape=jax.S...  6.69 us
    reshape x4, local copies, waits for them, and re-layouts, flat(): return value.reshape(lead + (DIRS * tiles, points))  4.69 us
    dynamic_slice x4, local copies, waits for them, and re-layouts, mine(): lax.dynamic_slice(value, (0, me * tiles), (12, tiles))  2.88 us
    ppermute x6, waiting for transfers between devices, moved_targets(): came = lax.ppermute(slab, name, links)  2.32 us
  transfers between devices with their start and end apart: 6, of which 2 were waited for; matrix products, arithmetic and copies ran while one was open for 8% of the time, Pallas kernels for 0%

profile of v3, /device:TPU:15, one launch (start us, length us, event | category | flops | bytes accessed | tf_op | source)
XLA Modules:
  0.0 103.4 jit_solution(17146380054341921356)
XLA Ops:
  0.7 1.4 %fusion.21 = (f32[3,1,1,4,2,512]{5,4,3,2,1,0:T(2,128)S(1)}, f32[3,1,1,4,2,512]{5,4,3,2,1,0:T(2,128)S(1)}, f32[3,1,1,4,2,512]{5,4,3,2,1,0:T(2,128)S(1)}, f32[3,1,...) fusion(f32[3,13,1,4,2,512]{5,4,3,2,1,0:T(2,128)} %param.16), kind=kLoop, calls=%fused_computation.143 | loop fusion | bytes 1277952 | tf_op jit(solution)/shard_map/slice | solution.py:64
  2.2 3.2 %collective-permute-start.1 = (f32[2,3,1,4,2,512]{5,4,1,3,2,0:T(2,128)S(1)}, f32[2,3,1,4,2,512]{5,4,1,3,2,0:T(2,128)S(1)}, u32[]{:S(2)}, u32[]{:S(2)}) collective-permute-start(f32[2,3,1,4,2,512]{5,4,1,3,2,0:T(2,128)S(1)} %pad_maximum_fusion), channel_id=1, source_target_pairs={{0,8},{8,16},{16,24},{1,9},{9,17},{17,25},{2,10},{10,18},{18,26},{... | collective-permute-start | bytes 294920 | tf_op jit(solution)/shard_map/ppermute | solution.py:81
  5.5 2.1 %collective-permute-start = (f32[7,3,1,4,2,512]{5,4,1,3,2,0:T(2,128)S(1)}, f32[7,3,1,4,2,512]{5,4,1,3,2,0:T(2,128)S(1)}, u32[]{:S(2)}, u32[]{:S(2)}) collective-permute-start(f32[7,3,1,4,2,512]{5,4,1,3,2,0:T(2,128)S(1)} %constant_dynamic-update-slice_fusion), channel_id=1, source_target_pairs={{8,0},{16,8},{24,16},{9,1},{17,9},{25,17},{10,2},{18,10},{26,18},{... | collective-permute-start | bytes 1032200 | tf_op jit(solution)/shard_map/ppermute | solution.py:81
  7.6 0.7 fusion.20
  8.3 0.7 and_convert_fusion
  9.0 0.7 fusion.19
  9.8 0.7 multiply_multiply_fusion
  10.5 0.1 copy.816
  10.6 0.1 reshape.116
  10.8 0.1 pad.12.clone
  11.6 0.1 copy.817
  11.7 0.7 pad.9.affine
  12.4 0.6 pad.8.lane_table
  13.0 0.8 reshape.115.weight
  13.8 1.3 %reshape.112.source = f32[3,104,512]{2,1,0:T(8,128)} reshape(f32[3,13,1,4,2,512]{5,4,3,2,1,0:T(2,128)S(1)} %copy-done) | data formatting | bytes 1277952 | tf_op jit(solution)/shard_map/reshape | solution.py:497
  15.1 1.3 %reshape.114.normal = f32[3,104,512]{2,1,0:T(8,128)} reshape(f32[3,13,1,4,2,512]{5,4,3,2,1,0:T(2,128)S(1)} %copy-done.1) | data formatting | bytes 1277952 | tf_op jit(solution)/shard_map/reshape | solution.py:497
  16.7 1.3 %collective-permute-start.3 = (f32[2,3,1,1,2,512]{5,4,1,3,2,0:T(2,128)S(1)}, f32[2,3,1,1,2,512]{5,4,1,3,2,0:T(2,128)S(1)}, u32[]{:S(2)}, u32[]{:S(2)}) collective-permute-start(f32[2,3,1,1,2,512]{5,4,1,3,2,0:T(2,128)S(1)} %pad_maximum_fusion.8), channel_id=1, source_target_pairs={{0,2},{2,4},{4,6},{1,3},{3,5},{5,7},{8,10},{10,12},{12,14},{9,11},... | collective-permute-start | bytes 73736 | tf_op jit(solution)/shard_map/ppermute | solution.py:81
  18.1 4.0 %collective-permute-start.2 = (f32[7,3,1,1,2,512]{5,4,1,3,2,0:T(2,128)S(1)}, f32[7,3,1,1,2,512]{5,4,1,3,2,0:T(2,128)S(1)}, u32[]{:S(2)}, u32[]{:S(2)}) collective-permute-start(f32[7,3,1,1,2,512]{5,4,1,3,2,0:T(2,128)S(1)} %constant_dynamic-update-slice_fusion.7), channel_id=1, source_target_pairs={{2,0},{4,2},{6,4},{3,1},{5,3},{7,5},{10,8},{12,10},{14,12},{11,9},... | collective-permute-start | bytes 258056 | tf_op jit(solution)/shard_map/ppermute | solution.py:81
  22.2 1.4 %collective-permute-done.2 = f32[7,3,1,1,2,512]{5,4,1,3,2,0:T(2,128)S(1)} collective-permute-done((f32[7,3,1,1,2,512]{5,4,1,3,2,0:T(2,128)S(1)}, f32[7,3,1,1,2,512]{5,4,1,3,2,0:T(2,128)S(1)}, u32[]{:S(2)}, u32[]{:S(2)}) %collective-permute-start.2) | collective-permute-done | bytes 86048 | tf_op jit(solution)/shard_map/ppermute | solution.py:81
  23.7 1.3 %collective-permute-start.5 = (f32[2,3,1,4,1,512]{5,3,1,4,2,0:T(4,128)S(1)}, f32[2,3,1,4,1,512]{5,3,1,4,2,0:T(4,128)S(1)}, u32[]{:S(2)}, u32[]{:S(2)}) collective-permute-start(f32[2,3,1,4,1,512]{5,3,1,4,2,0:T(4,128)S(1)} %pad_maximum_fusion.7), channel_id=1, source_target_pairs={{0,1},{2,3},{4,5},{6,7},{8,9},{10,11},{12,13},{14,15},{16,17},{18,... | collective-permute-start | bytes 147464 | tf_op jit(solution)/shard_map/ppermute | solution.py:81
  25.2 4.4 %collective-permute-start.4 = (f32[7,3,1,4,1,512]{5,3,1,4,2,0:T(4,128)S(1)}, f32[7,3,1,4,1,512]{5,3,1,4,2,0:T(4,128)S(1)}, u32[]{:S(2)}, u32[]{:S(2)}) collective-permute-start(f32[7,3,1,4,1,512]{5,3,1,4,2,0:T(4,128)S(1)} %constant_dynamic-update-slice_fusion.14), channel_id=1, source_target_pairs={{1,0},{3,2},{5,4},{7,6},{9,8},{11,10},{13,12},{15,14},{17,16},{19,... | collective-permute-start | bytes 516104 | tf_op jit(solution)/shard_map/ppermute | solution.py:81
  29.8 0.9 collective-permute-done.4
  31.6 0.4 copy.815
  32.0 1.3 %reshape.113.target = f32[3,104,512]{2,1,0:T(8,128)} reshape(f32[3,13,1,4,2,512]{5,4,3,1,0,2:T(2,128)S(1)} %copy.815) | data formatting | bytes 1277952 | tf_op jit(solution)/shard_map/reshape | solution.py:497
  33.2 6.7 %assemble.1.mine = f32[160,128]{1,0:T(8,128)} custom-call(f32[3,104,512]{2,1,0:T(8,128)} %reshape.112.source, f32[3,104,512]{2,1,0:T(8,128)} %reshape.113.target, f32[3,104,512]{2,1,0:T(8,128)} %reshape.114.normal, f32[104,512]{1,0:T(8,128)} %reshape.115.weight, f32[8,128]{1,0:T(8,128)} %pad.8.lane_table, f32[16,128]{1,0:T(8,128)} %pad.9.affine), custom_call_target="tpu_custom_call" | custom-call | tf_op jit(solution)/shard_map/assemble/pallas_call | solution.py:499
  39.9 39.8 %gather.1.gathered = f32[32,160,128]{2,1,0:T(8,128)} custom-call(f32[160,128]{1,0:T(8,128)} %assemble.1.mine), custom_call_target="tpu_custom_call" | custom-call | tf_op jit(solution)/shard_map/gather/pallas_call | solution.py:519
  79.7 7.6 %turn.1.parts = f32[16,160,256]{2,1,0:T(8,128)} custom-call(f32[32,160,128]{2,1,0:T(8,128)} %gather.1.gathered), custom_call_target="tpu_custom_call" | custom-call | tf_op jit(solution)/shard_map/turn/pallas_call | solution.py:528
  87.3 13.2 %solve.1 = (f32[16,256]{1,0:T(8,128)}, f32[16,256]{1,0:T(8,128)}) custom-call(s32[1]{0:T(128)S(6)} %copy.903.anchor, f32[16,160,256]{2,1,0:T(8,128)} %turn.1.parts, f32[16,256]{1,0:T(8,128)} %constant.54.clone.table), custom_call_target="tpu_custom_call" | custom-call | tf_op jit(solution)/shard_map/solve/pallas_call | solution.py:537
  100.5 0.8 constant_dynamic-slice_fusion.1
  101.3 0.8 constant_dynamic-slice_fusion
  102.1 0.7 copy.819
  102.7 0.7 copy.818
  (95 shorter events, 1.8 us)
Async XLA Ops:
  0.6 10.3 %copy-start.4 = (f32[3,104]{1,0:T(4,128)S(1)}, f32[3,104]{1,0:T(4,128)}, u32[]{:S(2)}) copy-start(f32[3,104]{1,0:T(4,128)} %constant.53.clone) | copy-start | bytes 3748
  0.6 11.0 %copy-start.3 = (f32[12,1,4,2]{0,3,2,1:T(2,128)S(1)}, f32[12,1,4,2]{0,3,2,1:T(2,128)}, u32[]{:S(2)}) copy-start(f32[12,1,4,2]{0,3,2,1:T(2,128)} %param.20) | copy-start | bytes 1156
  0.7 12.3 %copy-start.2 = (f32[13,1,4,2,512]{4,3,2,1,0:T(2,128)S(1)}, f32[13,1,4,2,512]{4,3,2,1,0:T(2,128)}, u32[]{:S(2)}) copy-start(f32[13,1,4,2,512]{4,3,2,1,0:T(2,128)} %param.18) | copy-start | bytes 638980
  0.7 13.2 %copy-start = (f32[3,13,1,4,2,512]{5,4,3,2,1,0:T(2,128)S(1)}, f32[3,13,1,4,2,512]{5,4,3,2,1,0:T(2,128)}, u32[]{:S(2)}) copy-start(f32[3,13,1,4,2,512]{5,4,3,2,1,0:T(2,128)} %param.15) | copy-start | bytes 1916932
  0.7 14.4 %copy-start.1 = (f32[3,13,1,4,2,512]{5,4,3,2,1,0:T(2,128)S(1)}, f32[3,13,1,4,2,512]{5,4,3,2,1,0:T(2,128)}, u32[]{:S(2)}) copy-start(f32[3,13,1,4,2,512]{5,4,3,2,1,0:T(2,128)} %param.17) | copy-start | bytes 1916932
  2.2 14.2 %collective-permute-start.1 = (f32[2,3,1,4,2,512]{5,4,1,3,2,0:T(2,128)S(1)}, f32[2,3,1,4,2,512]{5,4,1,3,2,0:T(2,128)S(1)}, u32[]{:S(2)}, u32[]{:S(2)}) collective-permute-start(f32[2,3,1,4,2,512]{5,4,1,3,2,0:T(2,128)S(1)} %pad_maximum_fusion), channel_id=1, source_target_pairs={{0,8},{8,16},{16,24},{1,9},{9,17},{17,25},{2,10},{10,18},{18,26},{... | collective-permute-start | bytes 294920 | tf_op jit(solution)/shard_map/ppermute | solution.py:81
  5.5 11.0 %collective-permute-start = (f32[7,3,1,4,2,512]{5,4,1,3,2,0:T(2,128)S(1)}, f32[7,3,1,4,2,512]{5,4,1,3,2,0:T(2,128)S(1)}, u32[]{:S(2)}, u32[]{:S(2)}) collective-permute-start(f32[7,3,1,4,2,512]{5,4,1,3,2,0:T(2,128)S(1)} %constant_dynamic-update-slice_fusion), channel_id=1, source_target_pairs={{8,0},{16,8},{24,16},{9,1},{17,9},{25,17},{10,2},{18,10},{26,18},{... | collective-permute-start | bytes 1032200 | tf_op jit(solution)/shard_map/ppermute | solution.py:81
  16.7 5.4 %collective-permute-start.3 = (f32[2,3,1,1,2,512]{5,4,1,3,2,0:T(2,128)S(1)}, f32[2,3,1,1,2,512]{5,4,1,3,2,0:T(2,128)S(1)}, u32[]{:S(2)}, u32[]{:S(2)}) collective-permute-start(f32[2,3,1,1,2,512]{5,4,1,3,2,0:T(2,128)S(1)} %pad_maximum_fusion.8), channel_id=1, source_target_pairs={{0,2},{2,4},{4,6},{1,3},{3,5},{5,7},{8,10},{10,12},{12,14},{9,11},... | collective-permute-start | bytes 73736 | tf_op jit(solution)/shard_map/ppermute | solution.py:81
  18.1 5.5 %collective-permute-start.2 = (f32[7,3,1,1,2,512]{5,4,1,3,2,0:T(2,128)S(1)}, f32[7,3,1,1,2,512]{5,4,1,3,2,0:T(2,128)S(1)}, u32[]{:S(2)}, u32[]{:S(2)}) collective-permute-start(f32[7,3,1,1,2,512]{5,4,1,3,2,0:T(2,128)S(1)} %constant_dynamic-update-slice_fusion.7), channel_id=1, source_target_pairs={{2,0},{4,2},{6,4},{3,1},{5,3},{7,5},{10,8},{12,10},{14,12},{11,9},... | collective-permute-start | bytes 258056 | tf_op jit(solution)/shard_map/ppermute | solution.py:81
  23.7 6.0 %collective-permute-start.5 = (f32[2,3,1,4,1,512]{5,3,1,4,2,0:T(4,128)S(1)}, f32[2,3,1,4,1,512]{5,3,1,4,2,0:T(4,128)S(1)}, u32[]{:S(2)}, u32[]{:S(2)}) collective-permute-start(f32[2,3,1,4,1,512]{5,3,1,4,2,0:T(4,128)S(1)} %pad_maximum_fusion.7), channel_id=1, source_target_pairs={{0,1},{2,3},{4,5},{6,7},{8,9},{10,11},{12,13},{14,15},{16,17},{18,... | collective-permute-start | bytes 147464 | tf_op jit(solution)/shard_map/ppermute | solution.py:81
  25.2 5.4 %collective-permute-start.4 = (f32[7,3,1,4,1,512]{5,3,1,4,2,0:T(4,128)S(1)}, f32[7,3,1,4,1,512]{5,3,1,4,2,0:T(4,128)S(1)}, u32[]{:S(2)}, u32[]{:S(2)}) collective-permute-start(f32[7,3,1,4,1,512]{5,3,1,4,2,0:T(4,128)S(1)} %constant_dynamic-update-slice_fusion.14), channel_id=1, source_target_pairs={{1,0},{3,2},{5,4},{7,6},{9,8},{11,10},{13,12},{15,14},{17,16},{19,... | collective-permute-start | bytes 516104 | tf_op jit(solution)/shard_map/ppermute | solution.py:81
